TPU v7x, 32 devices: a whole 2x2x4 slice. The times are simulated.
32 devices in a mesh: grp: 4 (over z), shard: 8 (over y, x, core).
Axes of the slice: x: 2, y: 2, z: 4, core: 2. Of those that a mesh axis runs over, the one named last changes fastest.
Arguments:
- latents: bfloat16 [4096, 1024], P(('grp', 'shard')), may hold values from -6 to 6
- head_weight: bfloat16 [1024, 1024], P('shard'), may hold values from -0.1875 to 0.1875
- norm_gain: float32 [1024], replicated, may hold values from 0.1 to 1.9
- color_head: bfloat16 [4, 256], replicated, may hold values from -1.5 to 1.5
- sample_points: float32 [2048, 192], P(('grp', 'shard')), may hold values from -1 to 1
- sample_spacing: float32 [2048, 64], P(('grp', 'shard')), may hold values from 0.002 to 0.02
- ray_targets: float32 [3, 2048], P(None, ('grp', 'shard')), may hold values from 0 to 1
- ray_scene: int32 [2048], P(('grp', 'shard')), may hold values from 0 to 31, as said below
Outputs:
- rendered_color: float32 [3, 2048], P(None, ('grp', 'shard'))
- loss: float32 [], replicated
- head_grad: float32 [1024, 1024], P('shard')
- norm_gain_grad: float32 [1024], replicated
- latent_grad: bfloat16 [4096, 1024], P(('grp', 'shard'))
Inputs may be any that keep to these rules, and one draw needn't show every extreme that they name: `ray_scene`: one scene, drawn from the seed, is named by exactly 8 rays of every device; no device names any scene more than 8 times; every scene is named by one ray or more, and the totals of the other scenes differ from one another by one at most.
All inputs are finite; a program needn't handle non-finite values.
Results may differ from a plain program's by a relative error of at most 0.017.
Values may be sent and summed in bfloat16 or wider, within the bound.
A program may use at most 64 MiB of HBM per device.

v0:
```python
import math

import jax
import jax.numpy as jnp
from jax import lax
from jax.sharding import PartitionSpec as P

norm_eps = 1e-06


def encode(sample_rows, field_width):
    column = jnp.arange(field_width)
    component = column % 3
    octave = (column // 6 % 8).astype(jnp.float32)
    frequency = jnp.exp2(octave) * math.pi
    phase_shift = (column // 3 % 2).astype(jnp.float32) * (0.5 * math.pi)
    picked = jnp.zeros((sample_rows.shape[0], field_width), jnp.float32)
    for coord in range(3):
        chosen = (component == coord).astype(jnp.float32)
        picked = picked + sample_rows[:, coord : coord + 1] * chosen[None, :]
    return jnp.sin(picked * frequency + phase_shift)


def point_rows(points, ray_depth):
    ray_number = points.shape[0]
    return (
        points.reshape(ray_number, 3, ray_depth)
        .transpose(0, 2, 1)
        .reshape(ray_number * ray_depth, 3)
    )


def render_rays(points, spacing, target, live_rays, scene_factor, w_first, w_second, color_head):
    ray_number, ray_depth = spacing.shape
    field_width = w_first.shape[0]
    fan_scale = field_width ** (-0.5)
    sample_rows = point_rows(points, ray_depth)
    h_zero = encode(sample_rows, field_width).astype(jnp.bfloat16)
    h_one = jax.nn.relu(
        jnp.dot(h_zero, w_first, preferred_element_type=jnp.float32) * fan_scale
    ).astype(jnp.bfloat16)
    h_two = jax.nn.relu(
        jnp.dot(h_one, w_second, preferred_element_type=jnp.float32) * fan_scale
    ).astype(jnp.bfloat16)
    raw_out = lax.dot_general(
        color_head, h_two, (((1,), (1,)), ((), ())), preferred_element_type=jnp.float32
    )
    density = jax.nn.softplus(raw_out[0]).reshape(ray_number, ray_depth)
    albedo = jax.nn.sigmoid(raw_out[1:4]).reshape(3, ray_number, ray_depth)
    optical = density * spacing
    optical_before = jnp.cumsum(optical, axis=1) - optical
    transmit = jnp.exp(-optical_before)
    survive = jnp.exp(-optical)
    blend = transmit * (1.0 - survive)
    ray_color = jnp.sum(blend[None] * (albedo - 1.0), axis=2) + 1.0
    residual = ray_color - target.T
    loss_part = jnp.sum(
        jnp.where(live_rays, jnp.sum(residual * residual, axis=0) * scene_factor, 0.0)
    )
    grad_color = jnp.where(live_rays[None, :], 2.0 * residual * scene_factor, 0.0)
    d_albedo = grad_color[:, :, None] * blend[None]
    d_blend = jnp.sum(grad_color[:, :, None] * (albedo - 1.0), axis=0)
    weighted = d_blend * blend
    behind = jnp.sum(weighted, axis=1, keepdims=True) - jnp.cumsum(weighted, axis=1)
    d_optical = d_blend * transmit * survive - behind
    d_density = (
        d_optical * spacing * jax.nn.sigmoid(raw_out[0]).reshape(ray_number, ray_depth)
    ).reshape(1, ray_number * ray_depth)
    d_tint = (d_albedo * albedo * (1.0 - albedo)).reshape(3, ray_number * ray_depth)
    d_raw = jnp.concatenate([d_density, d_tint], axis=0).astype(jnp.bfloat16)
    d_htwo = lax.dot_general(
        d_raw, color_head, (((0,), (0,)), ((), ())), preferred_element_type=jnp.float32
    )
    d_atwo = (jnp.where(h_two > 0, d_htwo, 0.0) * fan_scale).astype(jnp.bfloat16)
    grad_second = lax.dot_general(
        h_one, d_atwo, (((0,), (0,)), ((), ())), preferred_element_type=jnp.float32
    )
    d_hone = lax.dot_general(
        d_atwo, w_second, (((1,), (1,)), ((), ())), preferred_element_type=jnp.float32
    )
    d_aone = (jnp.where(h_one > 0, d_hone, 0.0) * fan_scale).astype(jnp.bfloat16)
    grad_first = lax.dot_general(
        h_zero, d_aone, (((0,), (0,)), ((), ())), preferred_element_type=jnp.float32
    )
    return (ray_color, loss_part, grad_first, grad_second)


def body(
    latents,
    head_weight,
    norm_gain,
    color_head,
    sample_points,
    sample_spacing,
    ray_targets,
    ray_scene,
):
    devices = lax.axis_size(("grp", "shard"))
    ray_count, ray_depth = sample_spacing.shape
    tokens, model = latents.shape
    field_width = color_head.shape[1]
    per_layer = field_width * field_width // model
    per_device = 4 * ray_count // devices
    slot_total = per_device * devices
    latent_f32 = latents.astype(jnp.float32)
    inv_rms = lax.rsqrt(jnp.mean(latent_f32 * latent_f32, axis=1, keepdims=True) + norm_eps)
    x_hat = latent_f32 * inv_rms
    x_norm = (x_hat * norm_gain).astype(jnp.bfloat16)
    columns = x_norm
    field_sum = jnp.dot(
        columns,
        lax.all_gather(head_weight, "shard", axis=0, tiled=True),
        preferred_element_type=jnp.float32,
    )
    field_rows = field_sum.astype(jnp.bfloat16)
    w_first = field_rows[:per_layer].reshape(field_width, field_width)
    w_second = field_rows[per_layer:].reshape(field_width, field_width)
    ray_ids = jnp.arange(ray_count, dtype=jnp.int32)
    same_scene = ray_scene[:, None] == ray_scene[None, :]
    earlier = ray_ids[:, None] < ray_ids[None, :]
    ray_rank = jnp.sum(jnp.logical_and(same_scene, earlier).astype(jnp.int32), axis=0)
    slot_of_ray = ray_scene * per_device + ray_rank
    payload = jnp.concatenate([sample_points, sample_spacing], axis=1)
    send_payload = (
        jnp.zeros((slot_total, payload.shape[1]), jnp.float32).at[slot_of_ray].set(payload)
    )
    send_target = jnp.zeros((slot_total, 3), jnp.float32).at[slot_of_ray].set(ray_targets.T)
    send_live = jnp.zeros((slot_total,), jnp.float32).at[slot_of_ray].set(1.0)
    recv_payload, recv_target, recv_live = (
        lax.all_to_all(send_payload, ("grp", "shard"), split_axis=0, concat_axis=0, tiled=True),
        lax.all_to_all(send_target, ("grp", "shard"), split_axis=0, concat_axis=0, tiled=True),
        lax.all_to_all(send_live, ("grp", "shard"), split_axis=0, concat_axis=0, tiled=True),
    )
    block_rays = 1024 // ray_depth
    block_total = slot_total // block_rays
    scene_rays = jnp.sum(recv_live)
    scene_factor = 1.0 / (devices * scene_rays)

    def render_block(running, block_item):
        grad_first, grad_second, loss_sum = running
        block_payload, block_target, block_live = block_item
        ray_color, loss_part, more_first, more_second = render_rays(
            block_payload[:, : 3 * ray_depth],
            block_payload[:, 3 * ray_depth :],
            block_target,
            block_live > 0.5,
            scene_factor,
            w_first,
            w_second,
            color_head,
        )
        return (
            (grad_first + more_first, grad_second + more_second, loss_sum + loss_part),
            ray_color,
        )

    zero_grad = jnp.zeros((field_width, field_width), jnp.float32)
    block_items = (
        recv_payload.reshape(block_total, block_rays, payload.shape[1]),
        recv_target.reshape(block_total, block_rays, 3),
        recv_live.reshape(block_total, block_rays),
    )
    (grad_first, grad_second, loss_sum), block_colors = lax.scan(
        render_block, (zero_grad, zero_grad, jnp.zeros((), jnp.float32)), block_items
    )
    slot_colors = block_colors.transpose(1, 0, 2).reshape(3, slot_total)
    returned = lax.all_to_all(
        slot_colors, ("grp", "shard"), split_axis=1, concat_axis=1, tiled=True
    )
    rendered = returned[:, slot_of_ray]
    d_field = jnp.concatenate(
        [grad_first.reshape(per_layer, model), grad_second.reshape(per_layer, model)], axis=0
    ).astype(jnp.bfloat16)
    d_norm = lax.dot_general(
        d_field,
        lax.all_gather(head_weight, "shard", axis=0, tiled=True),
        (((1,), (1,)), ((), ())),
        preferred_element_type=jnp.float32,
    )
    columns = x_norm
    group_part = lax.psum_scatter(
        lax.dot_general(
            columns, d_field, (((0,), (0,)), ((), ())), preferred_element_type=jnp.float32
        ).astype(jnp.bfloat16),
        "shard",
        scatter_dimension=0,
        tiled=True,
    )
    head_grad = lax.psum(group_part, "grp").astype(jnp.float32)
    gain_part = jnp.sum(d_norm * x_hat, axis=0)
    norm_gain_grad, loss_total = lax.psum((gain_part, loss_sum), ("grp", "shard"))
    d_scaled = d_norm * norm_gain
    latent_grad = (
        inv_rms * (d_scaled - x_hat * jnp.mean(d_scaled * x_hat, axis=1, keepdims=True))
    ).astype(jnp.bfloat16)
    return (rendered, loss_total, head_grad, norm_gain_grad, latent_grad)


def solution(mesh):
    placed = (
        P(("grp", "shard"), None),
        P("shard", None),
        P(),
        P(),
        P(("grp", "shard"), None),
        P(("grp", "shard"), None),
        P(None, ("grp", "shard")),
        P(("grp", "shard")),
    )
    return jax.shard_map(
        body,
        mesh=mesh,
        in_specs=placed,
        out_specs=(
            P(None, ("grp", "shard")),
            P(),
            P("shard", None),
            P(),
            P(("grp", "shard"), None),
        ),
        check_vma=False,
    )
```

profile of v0, /device:TPU:0, one launch (start us, length us, event | category | flops | bytes accessed | tf_op | source)
XLA Modules:
  0.0 360.1 jit_solution(17849473619523795206)
XLA Ops:
  10.9 7.3 %all-to-all-start.1 = ((f32[32,8,1]{1,2,0:T(1,128)}), f32[32,8,1]{1,2,0:T(1,128)S(1)}, u32[]{:S(2)}, u32[]{:S(2)}) async-start(f32[32,8,1]{1,2,0:T(1,128)} %bitcast.2), calls=%async_computation.1 | async-start | bytes 32768 | tf_op jit(solution)/shard_map/all_to_all | solution.py:132
  32.1 4.9 %all-to-all-done.2 = f32[32,8,3]{1,2,0:T(4,128)S(1)} async-done(((f32[32,8,3]{1,2,0:T(4,128)}), f32[32,8,3]{1,2,0:T(4,128)S(1)}, u32[]{:S(2)}, u32[]{:S(2)}) %all-to-all-start.2) | async-done | bytes 3104 | tf_op jit(solution)/shard_map/all_to_all | solution.py:131
  43.4 6.9 %all-to-all-done = f32[32,8,256]{2,1,0:T(8,128)S(1)} async-done(((f32[32,8,256]{2,1,0:T(8,128)}), f32[32,8,256]{2,1,0:T(8,128)S(1)}, u32[]{:S(2)}, u32[]{:S(2)}) %all-to-all-start) | async-done | bytes 262176 | tf_op jit(solution)/shard_map/all_to_all | solution.py:130
  50.3 210.9 %while.20 = (s32[]{:T(128)}, f32[256,256]{1,0:T(8,128)S(1)}, f32[256,256]{1,0:T(8,128)S(1)}, f32[]{:T(128)}, f32[16,3,16]{2,1,0:T(4,128)S(1)}, /*index=5*/f32[16...) while((s32[]{:T(128)}, f32[256,256]{1,0:T(8,128)S(1)}, ...), condition=%wide.region_14.15_spmd.clone, body=%wide.region_6.14_spmd.clone.sunk | while | flops 683649216 | bytes 7148784 | solution.py:163
  50.6 4.6 %fusion.109 = bf16[1024,256]{1,0:T(8,128)(2,1)S(1)} fusion(bf16[256,256]{1,0:T(8,128)(2,1)S(1)} %get-tuple-element.516, f32[256]{0:T(256)S(1)} %get-tuple-element.465, f32[256]{0:T(256)S(1)} %get-tuple-element.466, f32[256]{0:T(256)S(1)} %get-tuple-element.467, f32[1024]{0:T(1024)S(1)} %bitcast.98, f32[256]{0:T(256)S(1)} %get-tuple-element.469, ...), kind=kOutput, calls=%fused_computation.12.clone.1 | convolution fusion | flops 137101312 | bytes 672768 | tf_op jit(solution)/shard_map/while/body/eval_jaxpr/dot_general | solution.py:40
  58.6 4.2 %fusion.114 = f32[256,256]{1,0:T(8,128)S(1)} fusion(bf16[1024,256]{1,0:T(8,128)(2,1)S(1)} %fusion.113, bf16[256,256]{1,0:T(8,128)(2,1)S(1)} %get-tuple-element.517, bf16[1024,256]{1,0:T(8,128)(2,1)S(1)} %fusion.109, f32[256,256]{1,0:T(8,128)S(1)} %get-tuple-element.495, f32[256]{0:T(256)S(1)} %get-tuple-element.465, f32[256]{0:T(256)S(1)} %get-tuple-element.466, ...), kind=kOutput, calls=%fused_computation.17.clone.1 | convolution fusion | flops 271712256 | bytes 1721345 | tf_op jit(solution)/shard_map/while/body/eval_jaxpr/dot_general | solution.py:82
  63.8 4.6 %fusion.109 = bf16[1024,256]{1,0:T(8,128)(2,1)S(1)} fusion(bf16[256,256]{1,0:T(8,128)(2,1)S(1)} %get-tuple-element.516, f32[256]{0:T(256)S(1)} %get-tuple-element.465, f32[256]{0:T(256)S(1)} %get-tuple-element.466, f32[256]{0:T(256)S(1)} %get-tuple-element.467, f32[1024]{0:T(1024)S(1)} %bitcast.98, f32[256]{0:T(256)S(1)} %get-tuple-element.469, ...), kind=kOutput, calls=%fused_computation.12.clone.1 | convolution fusion | flops 137101312 | bytes 672768 | tf_op jit(solution)/shard_map/while/body/eval_jaxpr/dot_general | solution.py:40
  71.8 4.2 %fusion.114 = f32[256,256]{1,0:T(8,128)S(1)} fusion(bf16[1024,256]{1,0:T(8,128)(2,1)S(1)} %fusion.113, bf16[256,256]{1,0:T(8,128)(2,1)S(1)} %get-tuple-element.517, bf16[1024,256]{1,0:T(8,128)(2,1)S(1)} %fusion.109, f32[256,256]{1,0:T(8,128)S(1)} %get-tuple-element.495, f32[256]{0:T(256)S(1)} %get-tuple-element.465, f32[256]{0:T(256)S(1)} %get-tuple-element.466, ...), kind=kOutput, calls=%fused_computation.17.clone.1 | convolution fusion | flops 271712256 | bytes 1721345 | tf_op jit(solution)/shard_map/while/body/eval_jaxpr/dot_general | solution.py:82
  76.9 4.6 %fusion.109 = bf16[1024,256]{1,0:T(8,128)(2,1)S(1)} fusion(bf16[256,256]{1,0:T(8,128)(2,1)S(1)} %get-tuple-element.516, f32[256]{0:T(256)S(1)} %get-tuple-element.465, f32[256]{0:T(256)S(1)} %get-tuple-element.466, f32[256]{0:T(256)S(1)} %get-tuple-element.467, f32[1024]{0:T(1024)S(1)} %bitcast.98, f32[256]{0:T(256)S(1)} %get-tuple-element.469, ...), kind=kOutput, calls=%fused_computation.12.clone.1 | convolution fusion | flops 137101312 | bytes 672768 | tf_op jit(solution)/shard_map/while/body/eval_jaxpr/dot_general | solution.py:40
  85.0 4.2 %fusion.114 = f32[256,256]{1,0:T(8,128)S(1)} fusion(bf16[1024,256]{1,0:T(8,128)(2,1)S(1)} %fusion.113, bf16[256,256]{1,0:T(8,128)(2,1)S(1)} %get-tuple-element.517, bf16[1024,256]{1,0:T(8,128)(2,1)S(1)} %fusion.109, f32[256,256]{1,0:T(8,128)S(1)} %get-tuple-element.495, f32[256]{0:T(256)S(1)} %get-tuple-element.465, f32[256]{0:T(256)S(1)} %get-tuple-element.466, ...), kind=kOutput, calls=%fused_computation.17.clone.1 | convolution fusion | flops 271712256 | bytes 1721345 | tf_op jit(solution)/shard_map/while/body/eval_jaxpr/dot_general | solution.py:82
  90.1 4.6 %fusion.109 = bf16[1024,256]{1,0:T(8,128)(2,1)S(1)} fusion(bf16[256,256]{1,0:T(8,128)(2,1)S(1)} %get-tuple-element.516, f32[256]{0:T(256)S(1)} %get-tuple-element.465, f32[256]{0:T(256)S(1)} %get-tuple-element.466, f32[256]{0:T(256)S(1)} %get-tuple-element.467, f32[1024]{0:T(1024)S(1)} %bitcast.98, f32[256]{0:T(256)S(1)} %get-tuple-element.469, ...), kind=kOutput, calls=%fused_computation.12.clone.1 | convolution fusion | flops 137101312 | bytes 672768 | tf_op jit(solution)/shard_map/while/body/eval_jaxpr/dot_general | solution.py:40
  103.3 4.6 %fusion.109 = bf16[1024,256]{1,0:T(8,128)(2,1)S(1)} fusion(bf16[256,256]{1,0:T(8,128)(2,1)S(1)} %get-tuple-element.516, f32[256]{0:T(256)S(1)} %get-tuple-element.465, f32[256]{0:T(256)S(1)} %get-tuple-element.466, f32[256]{0:T(256)S(1)} %get-tuple-element.467, f32[1024]{0:T(1024)S(1)} %bitcast.98, f32[256]{0:T(256)S(1)} %get-tuple-element.469, ...), kind=kOutput, calls=%fused_computation.12.clone.1 | convolution fusion | flops 137101312 | bytes 672768 | tf_op jit(solution)/shard_map/while/body/eval_jaxpr/dot_general | solution.py:40
  111.3 4.2 %fusion.114 = f32[256,256]{1,0:T(8,128)S(1)} fusion(bf16[1024,256]{1,0:T(8,128)(2,1)S(1)} %fusion.113, bf16[256,256]{1,0:T(8,128)(2,1)S(1)} %get-tuple-element.517, bf16[1024,256]{1,0:T(8,128)(2,1)S(1)} %fusion.109, f32[256,256]{1,0:T(8,128)S(1)} %get-tuple-element.495, f32[256]{0:T(256)S(1)} %get-tuple-element.465, f32[256]{0:T(256)S(1)} %get-tuple-element.466, ...), kind=kOutput, calls=%fused_computation.17.clone.1 | convolution fusion | flops 271712256 | bytes 1721345 | tf_op jit(solution)/shard_map/while/body/eval_jaxpr/dot_general | solution.py:82
  116.5 4.6 %fusion.109 = bf16[1024,256]{1,0:T(8,128)(2,1)S(1)} fusion(bf16[256,256]{1,0:T(8,128)(2,1)S(1)} %get-tuple-element.516, f32[256]{0:T(256)S(1)} %get-tuple-element.465, f32[256]{0:T(256)S(1)} %get-tuple-element.466, f32[256]{0:T(256)S(1)} %get-tuple-element.467, f32[1024]{0:T(1024)S(1)} %bitcast.98, f32[256]{0:T(256)S(1)} %get-tuple-element.469, ...), kind=kOutput, calls=%fused_computation.12.clone.1 | convolution fusion | flops 137101312 | bytes 672768 | tf_op jit(solution)/shard_map/while/body/eval_jaxpr/dot_general | solution.py:40
  129.7 4.6 %fusion.109 = bf16[1024,256]{1,0:T(8,128)(2,1)S(1)} fusion(bf16[256,256]{1,0:T(8,128)(2,1)S(1)} %get-tuple-element.516, f32[256]{0:T(256)S(1)} %get-tuple-element.465, f32[256]{0:T(256)S(1)} %get-tuple-element.466, f32[256]{0:T(256)S(1)} %get-tuple-element.467, f32[1024]{0:T(1024)S(1)} %bitcast.98, f32[256]{0:T(256)S(1)} %get-tuple-element.469, ...), kind=kOutput, calls=%fused_computation.12.clone.1 | convolution fusion | flops 137101312 | bytes 672768 | tf_op jit(solution)/shard_map/while/body/eval_jaxpr/dot_general | solution.py:40
  137.7 4.2 %fusion.114 = f32[256,256]{1,0:T(8,128)S(1)} fusion(bf16[1024,256]{1,0:T(8,128)(2,1)S(1)} %fusion.113, bf16[256,256]{1,0:T(8,128)(2,1)S(1)} %get-tuple-element.517, bf16[1024,256]{1,0:T(8,128)(2,1)S(1)} %fusion.109, f32[256,256]{1,0:T(8,128)S(1)} %get-tuple-element.495, f32[256]{0:T(256)S(1)} %get-tuple-element.465, f32[256]{0:T(256)S(1)} %get-tuple-element.466, ...), kind=kOutput, calls=%fused_computation.17.clone.1 | convolution fusion | flops 271712256 | bytes 1721345 | tf_op jit(solution)/shard_map/while/body/eval_jaxpr/dot_general | solution.py:82
  142.8 4.6 %fusion.109 = bf16[1024,256]{1,0:T(8,128)(2,1)S(1)} fusion(bf16[256,256]{1,0:T(8,128)(2,1)S(1)} %get-tuple-element.516, f32[256]{0:T(256)S(1)} %get-tuple-element.465, f32[256]{0:T(256)S(1)} %get-tuple-element.466, f32[256]{0:T(256)S(1)} %get-tuple-element.467, f32[1024]{0:T(1024)S(1)} %bitcast.98, f32[256]{0:T(256)S(1)} %get-tuple-element.469, ...), kind=kOutput, calls=%fused_computation.12.clone.1 | convolution fusion | flops 137101312 | bytes 672768 | tf_op jit(solution)/shard_map/while/body/eval_jaxpr/dot_general | solution.py:40
  156.0 4.6 %fusion.109 = bf16[1024,256]{1,0:T(8,128)(2,1)S(1)} fusion(bf16[256,256]{1,0:T(8,128)(2,1)S(1)} %get-tuple-element.516, f32[256]{0:T(256)S(1)} %get-tuple-element.465, f32[256]{0:T(256)S(1)} %get-tuple-element.466, f32[256]{0:T(256)S(1)} %get-tuple-element.467, f32[1024]{0:T(1024)S(1)} %bitcast.98, f32[256]{0:T(256)S(1)} %get-tuple-element.469, ...), kind=kOutput, calls=%fused_computation.12.clone.1 | convolution fusion | flops 137101312 | bytes 672768 | tf_op jit(solution)/shard_map/while/body/eval_jaxpr/dot_general | solution.py:40
  164.1 4.2 %fusion.114 = f32[256,256]{1,0:T(8,128)S(1)} fusion(bf16[1024,256]{1,0:T(8,128)(2,1)S(1)} %fusion.113, bf16[256,256]{1,0:T(8,128)(2,1)S(1)} %get-tuple-element.517, bf16[1024,256]{1,0:T(8,128)(2,1)S(1)} %fusion.109, f32[256,256]{1,0:T(8,128)S(1)} %get-tuple-element.495, f32[256]{0:T(256)S(1)} %get-tuple-element.465, f32[256]{0:T(256)S(1)} %get-tuple-element.466, ...), kind=kOutput, calls=%fused_computation.17.clone.1 | convolution fusion | flops 271712256 | bytes 1721345 | tf_op jit(solution)/shard_map/while/body/eval_jaxpr/dot_general | solution.py:82
  169.2 4.6 %fusion.109 = bf16[1024,256]{1,0:T(8,128)(2,1)S(1)} fusion(bf16[256,256]{1,0:T(8,128)(2,1)S(1)} %get-tuple-element.516, f32[256]{0:T(256)S(1)} %get-tuple-element.465, f32[256]{0:T(256)S(1)} %get-tuple-element.466, f32[256]{0:T(256)S(1)} %get-tuple-element.467, f32[1024]{0:T(1024)S(1)} %bitcast.98, f32[256]{0:T(256)S(1)} %get-tuple-element.469, ...), kind=kOutput, calls=%fused_computation.12.clone.1 | convolution fusion | flops 137101312 | bytes 672768 | tf_op jit(solution)/shard_map/while/body/eval_jaxpr/dot_general | solution.py:40
  182.4 4.6 %fusion.109 = bf16[1024,256]{1,0:T(8,128)(2,1)S(1)} fusion(bf16[256,256]{1,0:T(8,128)(2,1)S(1)} %get-tuple-element.516, f32[256]{0:T(256)S(1)} %get-tuple-element.465, f32[256]{0:T(256)S(1)} %get-tuple-element.466, f32[256]{0:T(256)S(1)} %get-tuple-element.467, f32[1024]{0:T(1024)S(1)} %bitcast.98, f32[256]{0:T(256)S(1)} %get-tuple-element.469, ...), kind=kOutput, calls=%fused_computation.12.clone.1 | convolution fusion | flops 137101312 | bytes 672768 | tf_op jit(solution)/shard_map/while/body/eval_jaxpr/dot_general | solution.py:40
  190.4 4.2 %fusion.114 = f32[256,256]{1,0:T(8,128)S(1)} fusion(bf16[1024,256]{1,0:T(8,128)(2,1)S(1)} %fusion.113, bf16[256,256]{1,0:T(8,128)(2,1)S(1)} %get-tuple-element.517, bf16[1024,256]{1,0:T(8,128)(2,1)S(1)} %fusion.109, f32[256,256]{1,0:T(8,128)S(1)} %get-tuple-element.495, f32[256]{0:T(256)S(1)} %get-tuple-element.465, f32[256]{0:T(256)S(1)} %get-tuple-element.466, ...), kind=kOutput, calls=%fused_computation.17.clone.1 | convolution fusion | flops 271712256 | bytes 1721345 | tf_op jit(solution)/shard_map/while/body/eval_jaxpr/dot_general | solution.py:82
  195.6 4.6 %fusion.109 = bf16[1024,256]{1,0:T(8,128)(2,1)S(1)} fusion(bf16[256,256]{1,0:T(8,128)(2,1)S(1)} %get-tuple-element.516, f32[256]{0:T(256)S(1)} %get-tuple-element.465, f32[256]{0:T(256)S(1)} %get-tuple-element.466, f32[256]{0:T(256)S(1)} %get-tuple-element.467, f32[1024]{0:T(1024)S(1)} %bitcast.98, f32[256]{0:T(256)S(1)} %get-tuple-element.469, ...), kind=kOutput, calls=%fused_computation.12.clone.1 | convolution fusion | flops 137101312 | bytes 672768 | tf_op jit(solution)/shard_map/while/body/eval_jaxpr/dot_general | solution.py:40
  208.8 4.6 %fusion.109 = bf16[1024,256]{1,0:T(8,128)(2,1)S(1)} fusion(bf16[256,256]{1,0:T(8,128)(2,1)S(1)} %get-tuple-element.516, f32[256]{0:T(256)S(1)} %get-tuple-element.465, f32[256]{0:T(256)S(1)} %get-tuple-element.466, f32[256]{0:T(256)S(1)} %get-tuple-element.467, f32[1024]{0:T(1024)S(1)} %bitcast.98, f32[256]{0:T(256)S(1)} %get-tuple-element.469, ...), kind=kOutput, calls=%fused_computation.12.clone.1 | convolution fusion | flops 137101312 | bytes 672768 | tf_op jit(solution)/shard_map/while/body/eval_jaxpr/dot_general | solution.py:40
  216.8 4.2 %fusion.114 = f32[256,256]{1,0:T(8,128)S(1)} fusion(bf16[1024,256]{1,0:T(8,128)(2,1)S(1)} %fusion.113, bf16[256,256]{1,0:T(8,128)(2,1)S(1)} %get-tuple-element.517, bf16[1024,256]{1,0:T(8,128)(2,1)S(1)} %fusion.109, f32[256,256]{1,0:T(8,128)S(1)} %get-tuple-element.495, f32[256]{0:T(256)S(1)} %get-tuple-element.465, f32[256]{0:T(256)S(1)} %get-tuple-element.466, ...), kind=kOutput, calls=%fused_computation.17.clone.1 | convolution fusion | flops 271712256 | bytes 1721345 | tf_op jit(solution)/shard_map/while/body/eval_jaxpr/dot_general | solution.py:82
  221.9 4.6 %fusion.109 = bf16[1024,256]{1,0:T(8,128)(2,1)S(1)} fusion(bf16[256,256]{1,0:T(8,128)(2,1)S(1)} %get-tuple-element.516, f32[256]{0:T(256)S(1)} %get-tuple-element.465, f32[256]{0:T(256)S(1)} %get-tuple-element.466, f32[256]{0:T(256)S(1)} %get-tuple-element.467, f32[1024]{0:T(1024)S(1)} %bitcast.98, f32[256]{0:T(256)S(1)} %get-tuple-element.469, ...), kind=kOutput, calls=%fused_computation.12.clone.1 | convolution fusion | flops 137101312 | bytes 672768 | tf_op jit(solution)/shard_map/while/body/eval_jaxpr/dot_general | solution.py:40
  235.1 4.6 %fusion.109 = bf16[1024,256]{1,0:T(8,128)(2,1)S(1)} fusion(bf16[256,256]{1,0:T(8,128)(2,1)S(1)} %get-tuple-element.516, f32[256]{0:T(256)S(1)} %get-tuple-element.465, f32[256]{0:T(256)S(1)} %get-tuple-element.466, f32[256]{0:T(256)S(1)} %get-tuple-element.467, f32[1024]{0:T(1024)S(1)} %bitcast.98, f32[256]{0:T(256)S(1)} %get-tuple-element.469, ...), kind=kOutput, calls=%fused_computation.12.clone.1 | convolution fusion | flops 137101312 | bytes 672768 | tf_op jit(solution)/shard_map/while/body/eval_jaxpr/dot_general | solution.py:40
  243.2 4.2 %fusion.114 = f32[256,256]{1,0:T(8,128)S(1)} fusion(bf16[1024,256]{1,0:T(8,128)(2,1)S(1)} %fusion.113, bf16[256,256]{1,0:T(8,128)(2,1)S(1)} %get-tuple-element.517, bf16[1024,256]{1,0:T(8,128)(2,1)S(1)} %fusion.109, f32[256,256]{1,0:T(8,128)S(1)} %get-tuple-element.495, f32[256]{0:T(256)S(1)} %get-tuple-element.465, f32[256]{0:T(256)S(1)} %get-tuple-element.466, ...), kind=kOutput, calls=%fused_computation.17.clone.1 | convolution fusion | flops 271712256 | bytes 1721345 | tf_op jit(solution)/shard_map/while/body/eval_jaxpr/dot_general | solution.py:82
  248.3 4.6 %fusion.109 = bf16[1024,256]{1,0:T(8,128)(2,1)S(1)} fusion(bf16[256,256]{1,0:T(8,128)(2,1)S(1)} %get-tuple-element.516, f32[256]{0:T(256)S(1)} %get-tuple-element.465, f32[256]{0:T(256)S(1)} %get-tuple-element.466, f32[256]{0:T(256)S(1)} %get-tuple-element.467, f32[1024]{0:T(1024)S(1)} %bitcast.98, f32[256]{0:T(256)S(1)} %get-tuple-element.469, ...), kind=kOutput, calls=%fused_computation.12.clone.1 | convolution fusion | flops 137101312 | bytes 672768 | tf_op jit(solution)/shard_map/while/body/eval_jaxpr/dot_general | solution.py:40
  264.7 38.0 %reduce-scatter.2.cloned.1.call-done = bf16[128,1024]{1,0:T(8,128)(2,1)} async-done(((bf16[1024,1024]{1,0:T(8,128)(2,1)}), bf16[128,1024]{1,0:T(8,128)(2,1)}) %reduce-scatter.2.cloned.1.call-update) | async-done | bytes 262160 | tf_op jit(solution)/shard_map/reduce_scatter | solution.py:181
  303.4 4.6 %all-to-all-start.3 = ((f32[3,32,8]{2,0,1:T(4,128)}), f32[3,32,8]{2,0,1:T(4,128)S(1)}, u32[]{:S(2)}, u32[]{:S(2)}) async-start(f32[3,32,8]{2,0,1:T(4,128)} %copy.39), calls=%async_computation.3 | async-start | bytes 131072 | tf_op jit(solution)/shard_map/all_to_all | solution.py:167
  308.9 41.4 %all-reduce = (f32[]{:T(128)}, f32[1024]{0:T(1024)}) all-reduce(f32[]{:T(128)} %get-tuple-element.221, f32[1024]{0:T(1024)S(1)} %get-tuple-element.326), channel_id=1, replica_groups=mesh['grp'=4,'shard'=8] {'grp','shard'}, use_global_device_ids=true, to_apply=%region_15.16 | all-reduce | flops 1025 | bytes 8200 | tf_op jit(solution)/shard_map/psum | solution.py:191
  (612 shorter events, 119.1 us)
Async XLA Ops:
  7.2 33.9 %copy-start.1 = (bf16[128,1024]{1,0:T(8,128)(2,1)S(1)}, bf16[128,1024]{1,0:T(8,128)(2,1)}, u32[]{:S(2)}) copy-start(bf16[128,1024]{1,0:T(8,128)(2,1)} %param.10) | copy-start | bytes 786436
  7.2 33.9 %copy-start.2 = (f32[1024]{0:T(1024)S(1)}, f32[1024]{0:T(1024)}, u32[]{:S(2)}) copy-start(f32[1024]{0:T(1024)} %param.12) | copy-start | bytes 12292
  7.2 33.9 %all-gather.2.cloned.1.call-start = ((), (), s32[]{:S(2)}) async-start(), calls=%async_computation.5 | async-start | bytes 2359296 | tf_op jit(solution)/shard_map/all_gather | solution.py:112
  10.9 14.5 %all-to-all-start.1 = ((f32[32,8,1]{1,2,0:T(1,128)}), f32[32,8,1]{1,2,0:T(1,128)S(1)}, u32[]{:S(2)}, u32[]{:S(2)}) async-start(f32[32,8,1]{1,2,0:T(1,128)} %bitcast.2), calls=%async_computation.1 | async-start | bytes 32768 | tf_op jit(solution)/shard_map/all_to_all | solution.py:132
  25.4 11.6 %all-to-all-start.2 = ((f32[32,8,3]{1,2,0:T(4,128)}), f32[32,8,3]{1,2,0:T(4,128)S(1)}, u32[]{:S(2)}, u32[]{:S(2)}) async-start(f32[32,8,3]{1,2,0:T(4,128)} %copy.35), calls=%async_computation.2 | async-start | bytes 131072 | tf_op jit(solution)/shard_map/all_to_all | solution.py:131
  37.0 13.3 %copy-start.3 = (bf16[4,256]{1,0:T(4,128)(2,1)S(1)}, bf16[4,256]{1,0:T(4,128)(2,1)}, u32[]{:S(2)}) copy-start(bf16[4,256]{1,0:T(4,128)(2,1)} %param.13) | copy-start | bytes 6148
  37.0 13.3 %all-to-all-start = ((f32[32,8,256]{2,1,0:T(8,128)}), f32[32,8,256]{2,1,0:T(8,128)S(1)}, u32[]{:S(2)}, u32[]{:S(2)}) async-start(f32[32,8,256]{2,1,0:T(8,128)} %bitcast), calls=%async_computation | async-start | bytes 524288 | tf_op jit(solution)/shard_map/all_to_all | solution.py:130
  39.7 262.9 %reduce-scatter.2.cloned.1.call-start = ((), (), s32[]{:S(2)}) async-start(), calls=%async_computation.6 | async-start | bytes 2359296 | tf_op jit(solution)/shard_map/reduce_scatter | solution.py:181
  261.5 2.2 copy-start
  263.7 88.2 %all-reduce.3.cloned.1.call-start = ((), (), s32[]{:S(2)}) async-start(), calls=%async_computation.7 | async-start | bytes 524288 | tf_op jit(solution)/shard_map/psum | solution.py:189
  303.4 46.9 %all-to-all-start.3 = ((f32[3,32,8]{2,0,1:T(4,128)}), f32[3,32,8]{2,0,1:T(4,128)S(1)}, u32[]{:S(2)}, u32[]{:S(2)}) async-start(f32[3,32,8]{2,0,1:T(4,128)} %copy.39), calls=%async_computation.3 | async-start | bytes 131072 | tf_op jit(solution)/shard_map/all_to_all | solution.py:167
Sparse Core Ops, SparseCore 0:
  9.9 31.1 all-gather.1
  263.8 38.8 reduce-scatter.1
  305.0 35.4 all-reduce.2
where the time goes:
time: 361 us; the launch traced here: 360 us
  matrix products  167 us (46%)
  waiting for transfers between devices  53.5 us (15%)
  blocking collectives  41.4 us (11%)
  other arithmetic  33.4 us (9%)
  local copies, waits for them, and re-layouts  19.5 us (5%)
  starting transfers between devices  18.9 us (5%)
  between operations  14.7 us (4%)
  loops' own time  12.3 us (3%)
    dot_general x16, matrix products, render_rays(): jnp.dot(h_zero, w_first, preferred_element_type=jnp.float32) * fan_scale  73.2 us
    dot_general x16, matrix products, render_rays(): lax.dot_general(h_zero, d_aone, (((0,), (0,)), ((), ())), preferred_eleme...  67.2 us
    psum x1, blocking collectives, body(): lax.psum((gain_part, loss_sum), ('grp', 'shard'))  41.4 us
    reduce_scatter x1, waiting for transfers between devices, body(): lax.psum_scatter(lax.dot_general(columns, d_field, (((0,), (0,)), ((), ()...  38 us
    another operation x1, loops' own time, body(): lax.scan(render_block, (zero_grad, zero_grad, jnp.zeros((), jnp.float32))...  12.3 us
    reduce_sum x16, other arithmetic, render_rays(): jnp.sum(jnp.where(live_rays, jnp.sum(residual * residual, axis=0) * scene...  9.75 us
    all_to_all x1, starting transfers between devices, body(): lax.all_to_all(send_live, ('grp', 'shard'), split_axis=0, concat_axis=0,...  7.33 us
  transfers between devices with their start and end apart: 7, of which 5 were waited for; matrix products, arithmetic and copies ran while one was open for 4% of the time, Pallas kernels for 0%

commit v1 on v0

v1 whole, which is shorter than its diff:
```python
import functools

import jax
import jax.numpy as jnp
from jax import lax
from jax.experimental import pallas as pl
from jax.experimental.pallas import tpu as pltpu
from jax.sharding import PartitionSpec as P

norm_eps = 1e-06


LANES = 128
SINE = (3.14159265358979, -5.16771278004997, 2.55016403987735, -0.599264529320792, 0.0821458866111282, -0.00737043094571435, 0.000466302805767613, -0.0000219153534478303)


def sine_of_pi(turns):
    whole = jnp.floor(turns + 0.5)
    rest = turns - whole
    odd = whole - 2.0 * jnp.floor(whole * 0.5)
    square = rest * rest
    value = jnp.full_like(square, SINE[-1])
    for coefficient in SINE[-2::-1]:
        value = value * square + coefficient
    return value * (rest * (1.0 - 2.0 * odd))


def ray_kernel(
    ray_depth,
    points_ref,
    spacing_ref,
    target_ref,
    factor_ref,
    first_t_ref,
    second_t_ref,
    second_ref,
    head_ref,
    head_t_ref,
    color_ref,
    loss_ref,
    grad_first_ref,
    grad_second_ref,
    raw_ref,
    draw_ref,
):
    width = second_ref.shape[0]
    fan_scale = width ** (-0.5)
    samples = points_ref.shape[1]
    chunks = samples // LANES

    @pl.when(pl.program_id(0) == 0)
    def _():
        loss_ref[...] = jnp.zeros_like(loss_ref)
        grad_first_ref[...] = jnp.zeros_like(grad_first_ref)
        grad_second_ref[...] = jnp.zeros_like(grad_second_ref)
        draw_ref[...] = jnp.zeros_like(draw_ref)

    feature = lax.broadcasted_iota(jnp.int32, (48, 1), 0)
    component = feature % 3
    scale = jnp.exp2((feature // 6 % 8).astype(jnp.float32))
    phase = (feature // 3 % 2).astype(jnp.float32) * 0.5
    picked = jnp.where(
        component == 0,
        points_ref[0:1, :],
        jnp.where(component == 1, points_ref[1:2, :], points_ref[2:3, :]),
    )
    turns = picked * scale
    turns = turns - 2.0 * jnp.floor(turns * 0.5)
    distinct = sine_of_pi(turns + phase).astype(jnp.bfloat16)
    copies = width // 48
    h_zero = jnp.concatenate([distinct] * copies + [distinct[: width - 48 * copies]], axis=0)

    def product(a, b):
        return jnp.dot(a, b, preferred_element_type=jnp.float32)

    h_one = jnp.maximum(product(first_t_ref[...], h_zero) * fan_scale, 0.0).astype(jnp.bfloat16)
    h_two = jnp.maximum(product(second_t_ref[...], h_one) * fan_scale, 0.0).astype(jnp.bfloat16)
    raw = product(head_ref[...], h_two)
    for i in range(chunks):
        for c in range(4):
            raw_ref[c, i : i + 1, :] = raw[c : c + 1, i * LANES : (i + 1) * LANES]

    row = lax.broadcasted_iota(jnp.int32, (LANES, LANES), 0)
    column = lax.broadcasted_iota(jnp.int32, (LANES, LANES), 1)
    same = row // ray_depth == column // ray_depth
    before_sum = jnp.where(jnp.logical_and(same, row < column), 1.0, 0.0)
    behind_sum = jnp.where(jnp.logical_and(same, row > column), 1.0, 0.0)
    whole_sum = jnp.where(same, 1.0, 0.0)

    def along(values, matrix):
        return jnp.dot(
            values, matrix, preferred_element_type=jnp.float32, precision=lax.Precision.HIGHEST
        )

    spacing = spacing_ref[...]
    factor = factor_ref[...]
    density_raw = raw_ref[0]
    density = jnp.maximum(density_raw, 0.0) + jnp.log1p(jnp.exp(-jnp.abs(density_raw)))
    optical = density * spacing
    transmit = jnp.exp(-along(optical, before_sum))
    survive = jnp.exp(-optical)
    blend = transmit * (1.0 - survive)
    d_blend = jnp.zeros_like(blend)
    loss = jnp.zeros_like(blend)
    tints = []
    for c in range(3):
        albedo = 1.0 / (1.0 + jnp.exp(-raw_ref[c + 1]))
        color = along(blend * (albedo - 1.0), whole_sum) + 1.0
        color_ref[c] = color
        residual = color - target_ref[c]
        loss = loss + residual * residual
        grad_color = 2.0 * residual * factor
        d_blend = d_blend + grad_color * (albedo - 1.0)
        tints.append(grad_color * blend * albedo * (1.0 - albedo))
    loss_ref[...] += loss * factor
    behind = along(d_blend * blend, behind_sum)
    d_optical = d_blend * transmit * survive - behind
    d_density = d_optical * spacing * (1.0 / (1.0 + jnp.exp(-density_raw)))
    for c, value in enumerate([d_density] + tints):
        for i in range(chunks):
            draw_ref[c : c + 1, i * LANES : (i + 1) * LANES] = value[i : i + 1, :]
    d_raw = draw_ref[...].astype(jnp.bfloat16)
    d_htwo = product(head_t_ref[...], d_raw)
    d_atwo = (jnp.where(h_two > 0, d_htwo, 0.0) * fan_scale).astype(jnp.bfloat16)
    over_samples = (((1,), (1,)), ((), ()))
    grad_second_ref[...] += lax.dot_general(
        h_one, d_atwo, over_samples, preferred_element_type=jnp.float32
    )
    d_hone = product(second_ref[...], d_atwo)
    d_aone = (jnp.where(h_one > 0, d_hone, 0.0) * fan_scale).astype(jnp.bfloat16)
    grad_first_ref[...] += lax.dot_general(
        distinct, d_aone, over_samples, preferred_element_type=jnp.float32
    )


def render_slots(points, spacing, target, factor, w_first, w_second, color_head):
    slots, ray_depth = spacing.shape
    width = w_first.shape[0]
    total = slots * ray_depth
    block = 2048
    rows = total // LANES
    block_rows = block // LANES
    flat_points = points.reshape(slots, 3, ray_depth).transpose(1, 0, 2).reshape(3, total)
    wide_target = jnp.broadcast_to(target.T[:, :, None], (3, slots, ray_depth)).reshape(3, rows, LANES)
    wide_factor = jnp.broadcast_to(factor[:, None], (slots, ray_depth)).reshape(rows, LANES)
    head = jnp.pad(color_head, ((0, 16 - color_head.shape[0]), (0, 0)))
    fixed = lambda b: (0, 0)
    color, loss, grad_distinct, grad_second = pl.pallas_call(
        functools.partial(ray_kernel, ray_depth),
        grid=(total // block,),
        in_specs=[
            pl.BlockSpec((3, block), lambda b: (0, b)),
            pl.BlockSpec((block_rows, LANES), lambda b: (b, 0)),
            pl.BlockSpec((3, block_rows, LANES), lambda b: (0, b, 0)),
            pl.BlockSpec((block_rows, LANES), lambda b: (b, 0)),
            pl.BlockSpec((width, width), fixed),
            pl.BlockSpec((width, width), fixed),
            pl.BlockSpec((width, width), fixed),
            pl.BlockSpec((16, width), fixed),
            pl.BlockSpec((width, 16), fixed),
        ],
        out_specs=[
            pl.BlockSpec((3, block_rows, LANES), lambda b: (0, b, 0)),
            pl.BlockSpec((block_rows, LANES), fixed),
            pl.BlockSpec((48, width), fixed),
            pl.BlockSpec((width, width), fixed),
        ],
        out_shape=[
            jax.ShapeDtypeStruct((3, rows, LANES), jnp.float32),
            jax.ShapeDtypeStruct((block_rows, LANES), jnp.float32),
            jax.ShapeDtypeStruct((48, width), jnp.float32),
            jax.ShapeDtypeStruct((width, width), jnp.float32),
        ],
        scratch_shapes=[
            pltpu.VMEM((4, block_rows, LANES), jnp.float32),
            pltpu.VMEM((16, block), jnp.float32),
        ],
    )(
        flat_points,
        spacing.reshape(rows, LANES),
        wide_target,
        wide_factor,
        w_first.T,
        w_second.T,
        w_second,
        head,
        head.T,
    )
    colors = color.reshape(3, slots, ray_depth)[:, :, 0]
    copies = -(-width // 48)
    grad_first = jnp.tile(grad_distinct, (copies, 1))[:width]
    return colors, jnp.sum(loss) * (1.0 / ray_depth), grad_first, grad_second


def body(
    latents,
    head_weight,
    norm_gain,
    color_head,
    sample_points,
    sample_spacing,
    ray_targets,
    ray_scene,
):
    devices = lax.axis_size(("grp", "shard"))
    ray_count, ray_depth = sample_spacing.shape
    tokens, model = latents.shape
    field_width = color_head.shape[1]
    per_layer = field_width * field_width // model
    per_device = 4 * ray_count // devices
    slot_total = per_device * devices
    latent_f32 = latents.astype(jnp.float32)
    inv_rms = lax.rsqrt(jnp.mean(latent_f32 * latent_f32, axis=1, keepdims=True) + norm_eps)
    x_hat = latent_f32 * inv_rms
    x_norm = (x_hat * norm_gain).astype(jnp.bfloat16)
    columns = x_norm
    field_sum = jnp.dot(
        columns,
        lax.all_gather(head_weight, "shard", axis=0, tiled=True),
        preferred_element_type=jnp.float32,
    )
    field_rows = field_sum.astype(jnp.bfloat16)
    w_first = field_rows[:per_layer].reshape(field_width, field_width)
    w_second = field_rows[per_layer:].reshape(field_width, field_width)
    ray_ids = jnp.arange(ray_count, dtype=jnp.int32)
    same_scene = ray_scene[:, None] == ray_scene[None, :]
    earlier = ray_ids[:, None] < ray_ids[None, :]
    ray_rank = jnp.sum(jnp.logical_and(same_scene, earlier).astype(jnp.int32), axis=0)
    slot_of_ray = ray_scene * per_device + ray_rank
    payload = jnp.concatenate(
        [sample_points, sample_spacing, ray_targets.T, jnp.ones((ray_count, 1), jnp.float32)], axis=1
    )
    send = jnp.zeros((slot_total, payload.shape[1]), jnp.float32).at[slot_of_ray].set(payload)
    received = lax.all_to_all(send, ("grp", "shard"), split_axis=0, concat_axis=0, tiled=True)
    recv_points = received[:, : 3 * ray_depth]
    recv_spacing = received[:, 3 * ray_depth : 4 * ray_depth]
    recv_target = received[:, 4 * ray_depth : 4 * ray_depth + 3]
    recv_live = received[:, 4 * ray_depth + 3]
    scene_rays = jnp.sum(recv_live)
    scene_factor = 1.0 / (devices * scene_rays)

    slot_colors, loss_sum, grad_first, grad_second = render_slots(
        recv_points,
        recv_spacing,
        recv_target,
        recv_live * scene_factor,
        w_first,
        w_second,
        color_head,
    )
    returned = lax.all_to_all(
        slot_colors, ("grp", "shard"), split_axis=1, concat_axis=1, tiled=True
    )
    rendered = returned[:, slot_of_ray]
    d_field = jnp.concatenate(
        [grad_first.reshape(per_layer, model), grad_second.reshape(per_layer, model)], axis=0
    ).astype(jnp.bfloat16)
    d_norm = lax.dot_general(
        d_field,
        lax.all_gather(head_weight, "shard", axis=0, tiled=True),
        (((1,), (1,)), ((), ())),
        preferred_element_type=jnp.float32,
    )
    columns = x_norm
    group_part = lax.psum_scatter(
        lax.dot_general(
            columns, d_field, (((0,), (0,)), ((), ())), preferred_element_type=jnp.float32
        ).astype(jnp.bfloat16),
        "shard",
        scatter_dimension=0,
        tiled=True,
    )
    head_grad = jnp.sum(lax.all_gather(group_part, "grp", axis=0).astype(jnp.float32), axis=0)
    gain_part = jnp.sum(d_norm * x_hat, axis=0)
    norm_gain_grad, loss_total = lax.psum((gain_part, loss_sum), ("grp", "shard"))
    d_scaled = d_norm * norm_gain
    latent_grad = (
        inv_rms * (d_scaled - x_hat * jnp.mean(d_scaled * x_hat, axis=1, keepdims=True))
    ).astype(jnp.bfloat16)
    return (rendered, loss_total, head_grad, norm_gain_grad, latent_grad)


def solution(mesh):
    placed = (
        P(("grp", "shard"), None),
        P("shard", None),
        P(),
        P(),
        P(("grp", "shard"), None),
        P(("grp", "shard"), None),
        P(None, ("grp", "shard")),
        P(("grp", "shard")),
    )
    return jax.shard_map(
        body,
        mesh=mesh,
        in_specs=placed,
        out_specs=(
            P(None, ("grp", "shard")),
            P(),
            P("shard", None),
            P(),
            P(("grp", "shard"), None),
        ),
        check_vma=False,
    )
```

time: 361 us -> 183 us (0.51)
  matrix products: 167 us -> 5.12 us
  Pallas kernels: 0 us -> 29.1 us
  other arithmetic: 33.4 us -> 10.9 us
  loops' own time: 12.3 us -> 0 us
  local copies, waits for them, and re-layouts: 19.5 us -> 11.6 us
  starting transfers between devices: 18.9 us -> 12 us
    dot_general x96 -> x0, matrix products: 162 us -> none  [the longest x16 73.2 us: render_rays(): jnp.dot(h_zero, w_first, preferred_element_type=jnp.float32) * fan_scale]
    pallas_call x0 -> x1, Pallas kernels: none -> 29.1 us  [render_slots(): pl.pallas_call(functools.partial(ray_kernel, ray_depth), grid=(total // b...]
    another operation x1 -> x0, loops' own time: 12.3 us -> none  [body(): lax.scan(render_block, (zero_grad, zero_grad, jnp.zeros((), jnp.float32))...]
    reduce_sum x80 -> x2, other arithmetic: 14 us -> 2.85 us  [the longest x1 2.25 us: body(): jnp.sum(lax.all_gather(group_part, 'grp', axis=0).astype(jnp.float32), ax...]
    all_to_all x3 -> x1, starting transfers between devices: 14.1 us -> 7.33 us  [body(): lax.all_to_all(send, ('grp', 'shard'), split_axis=0, concat_axis=0, tiled...]
    another operation x50 -> x2, other arithmetic: 8.21 us -> 1.77 us  [the longest x16 3.53 us: render_rays(): optical_before = jnp.cumsum(optical, axis=1) - optical]
    all_gather x1, waiting for transfers between devices: 1.19 us -> 5.27 us  [body(): lax.all_gather(head_weight, 'shard', axis=0, tiled=True)]
    all_to_all x3 -> x1, waiting for transfers between devices: 13.6 us -> 9.92 us  [body(): lax.all_to_all(send, ('grp', 'shard'), split_axis=0, concat_axis=0, tiled...]
  transfers between devices with their start and end apart: 7 -> 5, of which waited for: 5 -> 3; matrix products, arithmetic and copies ran while one was open for 4% -> 10% of each run, Pallas kernels for 0% -> 0%
where the time goes in v1:
time: 183 us; the launch traced here: 182 us
  waiting for transfers between devices  57.1 us (31%)
  blocking collectives  40.9 us (22%)
  Pallas kernels  29.1 us (16%)
  between operations  15.3 us (8%)
  starting transfers between devices  12 us (7%)
  local copies, waits for them, and re-layouts  11.6 us (6%)
  other arithmetic  10.9 us (6%)
  matrix products  5.12 us (3%)
    reduce_scatter x1, waiting for transfers between devices, body(): lax.psum_scatter(lax.dot_general(columns, d_field, (((0,), (0,)), ((), ()...  41.2 us
    psum x1, blocking collectives, body(): lax.psum((gain_part, loss_sum), ('grp', 'shard'))  40.9 us
    pallas_call x1, Pallas kernels, render_slots(): pl.pallas_call(functools.partial(ray_kernel, ray_depth), grid=(total // b...  29.1 us
    all_to_all x1, waiting for transfers between devices, body(): lax.all_to_all(send, ('grp', 'shard'), split_axis=0, concat_axis=0, tiled...  9.92 us
    all_to_all x1, starting transfers between devices, body(): lax.all_to_all(send, ('grp', 'shard'), split_axis=0, concat_axis=0, tiled...  7.33 us
    all_gather x1, waiting for transfers between devices, body(): lax.all_gather(head_weight, 'shard', axis=0, tiled=True)  5.27 us
    all_to_all x1, starting transfers between devices, body(): lax.all_to_all(slot_colors, ('grp', 'shard'), split_axis=1, concat_axis=1...  4.59 us
  transfers between devices with their start and end apart: 5, of which 3 were waited for; matrix products, arithmetic and copies ran while one was open for 10% of the time, Pallas kernels for 0%

profile of v1, /device:TPU:0, one launch (start us, length us, event | category | flops | bytes accessed | tf_op | source)
XLA Modules:
  0.0 182.2 jit_solution(56692344443144682)
XLA Ops:
  7.2 0.7 all-gather.4.cloned.1.call-update
  7.9 0.8 copy.58
  8.7 0.8 convert_reduce_fusion.1
  9.6 0.7 compare_select_fusion
  10.2 1.9 %scatter_custom_fusion = f32[256,260]{1,0:T(8,128)} fusion(s32[64]{0:T(128)S(1)} %compare_select_fusion, f32[]{:T(128)} %constant.10.clone.1, f32[64,3]{1,0:T(8,128)S(1)} %copy.58, f32[]{:T(128)} %constant.31, f32[64,64]{1,0:T(8,128)} %param.13, f32[64,192]{1,0:T(8,128)} %param.12, f32[260]{0:T(512)S(1)} %pad.8.clone), kind=kCustom, calls=%fused_computation.19 | custom fusion | flops 49920 | bytes 366600 | tf_op jit(solution)/shard_map/scatter | solution.py:233
  12.2 7.3 %all-to-all-start = ((f32[32,8,260]{2,1,0:T(8,128)}), f32[32,8,260]{2,1,0:T(8,128)S(1)}, u32[]{:S(2)}, u32[]{:S(2)}) async-start(f32[32,8,260]{2,1,0:T(8,128)} %bitcast.1), calls=%async_computation | async-start | bytes 786432 | tf_op jit(solution)/shard_map/all_to_all | solution.py:234
  19.6 0.8 copy.64
  20.5 0.6 pad.4.clone.head_ref
  21.1 0.6 pad_bitcast_fusion.head_t_ref
  21.7 1.1 fusion.10
  22.8 9.9 %all-to-all-done = f32[32,8,260]{2,1,0:T(8,128)S(1)} async-done(((f32[32,8,260]{2,1,0:T(8,128)}), f32[32,8,260]{2,1,0:T(8,128)S(1)}, u32[]{:S(2)}, u32[]{:S(2)}) %all-to-all-start) | async-done | bytes 266272 | tf_op jit(solution)/shard_map/all_to_all | solution.py:234
  33.2 0.9 reshape.69.points_ref
  34.1 0.7 reshape.70.spacing_ref
  35.1 0.8 reshape.71.target_ref
  35.9 0.7 slice_reduce_fusion.1
  37.7 0.7 copy.65.factor_ref
  38.4 5.3 %all-gather.4.cloned.1.call-done = bf16[1024,1024]{1,0:T(8,128)(2,1)} async-done(((bf16[128,1024]{1,0:T(8,128)(2,1)}), bf16[1024,1024]{1,0:T(8,128)(2,1)}) %all-gather.4.cloned.1.call-update) | async-done | bytes 2097168 | tf_op jit(solution)/shard_map/all_gather | solution.py:219
  43.7 2.1 %convolution_convert_fusion.1 = bf16[128,1024]{1,0:T(8,128)(2,1)S(1)} fusion(bf16[1024,1024]{1,0:T(8,128)(2,1)} %all-gather.4.cloned.1.call-done, bf16[128,1024]{1,0:T(8,128)(2,1)S(1)} %copy-done.1, f32[1024]{0:T(1024)S(1)} %copy-done.4, f32[128]{0:T(128)S(1)} %add_rsqrt_fusion), kind=kOutput, calls=%fused_computation.4 | convolution fusion | flops 269090816 | bytes 2626048 | tf_op jit(solution)/shard_map/dot_general | solution.py:217
  45.9 0.8 copy.63
  46.7 0.7 copy.66.second_t_ref
  47.5 29.1 %shard_map.119 = (f32[3,128,128]{2,1,0:T(8,128)}, f32[16,128]{1,0:T(8,128)}, f32[48,256]{1,0:T(8,128)}, f32[256,256]{1,0:T(8,128)}) custom-call(f32[3,16384]{1,0:T(4,128)} %reshape.69.points_ref, f32[128,128]{1,0:T(8,128)} %reshape.70.spacing_ref, f32[3,128,128]{2,1,0:T(8,128)} %reshape.71.target_ref, f32[128,128]{1,0:T(8,128)} %copy.65.factor_ref, ...), custom_call_target="tpu_custom_call" | custom-call | tf_op jit(solution)/shard_map/pallas_call | solution.py:148
  76.6 0.8 convert.11
  77.6 1.0 convert.12
  78.7 2.1 %convolution_convert_fusion = bf16[1024,1024]{1,0:T(8,128)(2,1)} fusion(bf16[128,1024]{1,0:T(8,128)(2,1)S(1)} %constant_dynamic-update-slice_fusion, bf16[128,1024]{1,0:T(8,128)(2,1)S(1)} %copy-done.1, f32[1024]{0:T(1024)S(1)} %copy-done.4, f32[128]{0:T(128)S(1)} %add_rsqrt_fusion), kind=kOutput, calls=%fused_computation.3 | convolution fusion | flops 270008320 | bytes 2626048 | tf_op jit(solution)/shard_map/dot_general | solution.py:266
  80.8 41.2 %reduce-scatter.2.cloned.1.call-done = bf16[128,1024]{1,0:T(8,128)(2,1)} async-done(((bf16[1024,1024]{1,0:T(8,128)(2,1)}), bf16[128,1024]{1,0:T(8,128)(2,1)}) %reduce-scatter.2.cloned.1.call-update) | async-done | bytes 262160 | tf_op jit(solution)/shard_map/reduce_scatter | solution.py:265
  122.5 0.7 copy.68
  123.2 4.6 %all-to-all-start.1 = ((f32[3,32,8]{2,0,1:T(4,128)}), f32[3,32,8]{2,0,1:T(4,128)S(1)}, u32[]{:S(2)}, u32[]{:S(2)}) async-start(f32[3,32,8]{2,0,1:T(4,128)} %copy.68), calls=%async_computation.1 | async-start | bytes 131072 | tf_op jit(solution)/shard_map/all_to_all | solution.py:251
  127.8 0.9 fusion.6
  128.8 0.9 fusion.9
  131.0 40.9 %all-reduce.1 = (f32[]{:T(128)}, f32[1024]{0:T(1024)}) all-reduce(f32[]{:T(128)S(6)} %mul.70, f32[1024]{0:T(1024)S(1)} %get-tuple-element.39), channel_id=1, replica_groups=mesh['grp'=4,'shard'=8] {'grp','shard'}, use_global_device_ids=true, to_apply=%region_5.6 | all-reduce | flops 1025 | bytes 8200 | tf_op jit(solution)/shard_map/psum | solution.py:275
  172.7 0.7 copy.70
  173.4 2.3 %convert_reduce_fusion = f32[128,1024]{1,0:T(8,128)} fusion(bf16[4,128,1024]{2,1,0:T(8,128)(2,1)} %bitcast.29), kind=kLoop, calls=%fused_computation.2 | loop fusion | flops 917504 | bytes 1572864 | tf_op jit(solution)/shard_map/reduce_sum | solution.py:273
  (50 shorter events, 3.7 us)
Async XLA Ops:
  7.2 36.5 %all-gather.4.cloned.1.call-start = ((), (), s32[]{:S(2)}) async-start(), calls=%async_computation.3 | async-start | bytes 2359296 | tf_op jit(solution)/shard_map/all_gather | solution.py:219
  12.2 20.6 %all-to-all-start = ((f32[32,8,260]{2,1,0:T(8,128)}), f32[32,8,260]{2,1,0:T(8,128)S(1)}, u32[]{:S(2)}, u32[]{:S(2)}) async-start(f32[32,8,260]{2,1,0:T(8,128)} %bitcast.1), calls=%async_computation | async-start | bytes 786432 | tf_op jit(solution)/shard_map/all_to_all | solution.py:234
  19.5 102.6 %reduce-scatter.2.cloned.1.call-start = ((), (), s32[]{:S(2)}) async-start(), calls=%async_computation.4 | async-start | bytes 2359296 | tf_op jit(solution)/shard_map/reduce_scatter | solution.py:265
  32.8 10.9 %copy-start.1 = (bf16[128,1024]{1,0:T(8,128)(2,1)S(1)}, bf16[128,1024]{1,0:T(8,128)(2,1)}, u32[]{:S(2)}) copy-start(bf16[128,1024]{1,0:T(8,128)(2,1)} %param.8) | copy-start | bytes 786436
  32.8 10.9 %copy-start.4 = (f32[1024]{0:T(1024)S(1)}, f32[1024]{0:T(1024)}, u32[]{:S(2)}) copy-start(f32[1024]{0:T(1024)} %param.10) | copy-start | bytes 12292
  46.7 0.8 copy-start.2
  78.7 43.5 %copy-start.3 = (f32[3,128,128]{2,1,0:T(8,128)S(1)}, f32[3,128,128]{2,1,0:T(8,128)}, u32[]{:S(2)}) copy-start(f32[3,128,128]{2,1,0:T(8,128)} %get-tuple-element.9) | copy-start | bytes 589828
  80.8 47.0 %copy-start = (bf16[1024,1024]{1,0:T(8,128)(2,1)S(1)}, bf16[1024,1024]{1,0:T(8,128)(2,1)}, u32[]{:S(2)}) copy-start(bf16[1024,1024]{1,0:T(8,128)(2,1)} %all-gather.4.cloned.1.call-done) | copy-start | bytes 6291460
  80.8 92.6 %all-gather.6.cloned.1.call-start = ((), (), s32[]{:S(2)}) async-start(), calls=%async_computation.5 | async-start | bytes 1310720 | tf_op jit(solution)/shard_map/all_gather | solution.py:273
  123.2 48.7 %all-to-all-start.1 = ((f32[3,32,8]{2,0,1:T(4,128)}), f32[3,32,8]{2,0,1:T(4,128)S(1)}, u32[]{:S(2)}, u32[]{:S(2)}) async-start(f32[3,32,8]{2,0,1:T(4,128)} %copy.68), calls=%async_computation.1 | async-start | bytes 131072 | tf_op jit(solution)/shard_map/all_to_all | solution.py:251
  127.8 1.9 %copy-start.5 = (f32[16,128]{1,0:T(8,128)S(1)}, f32[16,128]{1,0:T(8,128)}, u32[]{:S(2)}) copy-start(f32[16,128]{1,0:T(8,128)} %get-tuple-element.10) | copy-start | bytes 24580
Sparse Core Ops, SparseCore 0:
  9.9 33.7 all-gather.3
  80.9 41.1 reduce-scatter.1
  123.7 28.1 all-gather.5

commit v2 on v1

--- a/solution.py
+++ b/solution.py
@@ -192,6 +192,290 @@
     return colors, jnp.sum(loss) * (1.0 / ray_depth), grad_first, grad_second
 
 
+MESH = pl.DeviceIdType.MESH
+
+
+def greet_all(groups, shards):
+    me = lax.axis_index("grp") * shards + lax.axis_index("shard")
+    total = groups * shards
+    barrier = pltpu.get_barrier_semaphore()
+
+    def greet(step, carry):
+        other = lax.rem(me + step, total)
+        pl.semaphore_signal(
+            barrier, inc=1, device_id=(other // shards, lax.rem(other, shards)), device_id_type=MESH
+        )
+        return carry
+
+    lax.fori_loop(1, total, greet, 0)
+    pl.semaphore_wait(barrier, total - 1)
+
+
+def messages(groups, shards, message_ref, landed, sent, arrived):
+    me = lax.axis_index("grp") * shards + lax.axis_index("shard")
+    total = groups * shards
+
+    def copy_to(step):
+        other = lax.rem(me + step, total)
+        return pltpu.make_async_remote_copy(
+            src_ref=message_ref.at[other],
+            dst_ref=landed.at[me],
+            send_sem=sent.at[other],
+            recv_sem=arrived.at[me],
+            device_id=(other // shards, lax.rem(other, shards)),
+            device_id_type=MESH,
+        )
+
+    def copy_from(step):
+        other = lax.rem(me + total - step, total)
+        return pltpu.make_async_remote_copy(
+            src_ref=message_ref.at[other],
+            dst_ref=landed.at[other],
+            send_sem=sent.at[other],
+            recv_sem=arrived.at[other],
+            device_id=(other // shards, lax.rem(other, shards)),
+            device_id_type=MESH,
+        )
+
+    def start():
+        def one(step, carry):
+            copy_to(step).start()
+            return carry
+
+        lax.fori_loop(1, total, one, 0)
+
+    def finish():
+        def one(step, carry):
+            copy_from(step).wait_recv()
+            copy_to(step).wait_send()
+            return carry
+
+        lax.fori_loop(1, total, one, 0)
+
+    return start, finish
+
+
+def tail_kernel(
+    groups,
+    shards,
+    message_ref,
+    turned_ref,
+    field_ref,
+    sums_ref,
+    colors_ref,
+    head_ref,
+    landed,
+    turned,
+    fields,
+    part,
+    parts,
+    done,
+    message_sent,
+    message_arrived,
+    turned_sent,
+    turned_arrived,
+    field_sent,
+    passed_on,
+    field_arrived,
+    part_sent,
+    part_arrived,
+    done_sent,
+    done_arrived,
+):
+    group = lax.axis_index("grp")
+    shard = lax.axis_index("shard")
+    me = group * shards + shard
+    chips = shards // 2
+    chip = shard // 2
+    core = lax.rem(shard, 2)
+    partner = chip * 2 + 1 - core
+
+    def remote(source, target, send_sem, recv_sem, to_group, to_shard):
+        return pltpu.make_async_remote_copy(
+            src_ref=source,
+            dst_ref=target,
+            send_sem=send_sem,
+            recv_sem=recv_sem,
+            device_id=(to_group, to_shard),
+            device_id_type=MESH,
+        )
+
+    def field_to(other):
+        return remote(
+            field_ref, fields.at[shard], field_sent.at[other], field_arrived.at[shard], group, other
+        )
+
+    def field_pass(origin):
+        return remote(
+            fields.at[origin],
+            fields.at[origin],
+            passed_on.at[origin],
+            field_arrived.at[origin],
+            group,
+            partner,
+        )
+
+    def turned_to(other):
+        return remote(
+            turned_ref.at[other],
+            turned.at[shard],
+            turned_sent.at[other],
+            turned_arrived.at[shard],
+            group,
+            other,
+        )
+
+    def turned_from(other):
+        return remote(
+            turned_ref.at[other],
+            turned.at[other],
+            turned_sent.at[other],
+            turned_arrived.at[other],
+            group,
+            other,
+        )
+
+    greet_all(groups, shards)
+    start_messages, finish_messages = messages(
+        groups, shards, message_ref, landed, message_sent, message_arrived
+    )
+    peers = [lax.rem(chip + step, chips) * 2 + core for step in range(1, chips)]
+    origins = [lax.rem(chip + chips - step, chips) * 2 + core for step in range(1, chips)]
+    others = [lax.rem(shard + step, shards) for step in range(1, shards)]
+    for other in peers:
+        field_to(other).start()
+    field_to(partner).start()
+    for other in others:
+        turned_to(other).start()
+    start_messages()
+
+    def product(rows, field):
+        return jnp.dot(rows, field, preferred_element_type=jnp.float32)
+
+    total = product(turned_ref[shard], field_ref[...])
+    field_pass(partner).wait_recv()
+    turned_from(partner).wait_recv()
+    total = total + product(turned[partner], fields[partner])
+    for origin in origins:
+        field_pass(origin).wait_recv()
+        field_pass(origin).start()
+        turned_from(origin).wait_recv()
+        total = total + product(turned[origin], fields[origin])
+    for origin in origins:
+        across = origin + 1 - 2 * core
+        field_pass(across).wait_recv()
+        turned_from(across).wait_recv()
+        total = total + product(turned[across], fields[across])
+
+    part[...] = total.astype(jnp.bfloat16).reshape(part.shape)
+    group_steps = [lax.rem(group + step, groups) for step in range(1, groups)]
+
+    def part_to(other):
+        return remote(
+            part.at[other], parts.at[group], part_sent.at[other], part_arrived.at[group], other, shard
+        )
+
+    def part_from(other):
+        return remote(
+            part.at[other], parts.at[other], part_sent.at[other], part_arrived.at[other], other, shard
+        )
+
+    def done_to(other):
+        return remote(
+            done.at[group], done.at[group], done_sent.at[other], done_arrived.at[group], other, shard
+        )
+
+    def done_from(other):
+        return remote(
+            done.at[other], done.at[other], done_sent.at[other], done_arrived.at[other], other, shard
+        )
+
+    for other in group_steps:
+        part_to(other).start()
+    slice_sum = part[group].astype(jnp.float32)
+    for other in group_steps:
+        part_from(other).wait_recv()
+        slice_sum = slice_sum + parts[other].astype(jnp.float32)
+    done[group] = slice_sum.astype(jnp.bfloat16)
+    for other in group_steps:
+        done_to(other).start()
+    head_ref[group] = slice_sum
+
+    finish_messages()
+    landed[me] = message_ref[me]
+    colors_ref[...] = landed[:, landed.shape[1] - 8 :, :]
+    sums_ref[...] = jnp.sum(landed[...], axis=0)
+
+    for other in group_steps:
+        done_from(other).wait_recv()
+        head_ref[other] = done[other].astype(jnp.float32)
+    for other in peers:
+        field_to(other).wait_send()
+    field_to(partner).wait_send()
+    for origin in origins:
+        field_pass(origin).wait_send()
+    for other in others:
+        turned_to(other).wait_send()
+    for other in group_steps:
+        part_to(other).wait_send()
+        done_to(other).wait_send()
+
+
+def tail_exchange(groups, shards, x_norm, d_field, gain_part, loss_sum, slot_colors):
+    tokens, model = x_norm.shape
+    devices = groups * shards
+    rows = model // shards
+    gain_rows = model // LANES
+    per_device = slot_colors.shape[1] // devices
+    turned = x_norm.T.reshape(shards, rows, tokens)
+    shared = jnp.concatenate(
+        [gain_part.reshape(gain_rows, LANES), jnp.broadcast_to(loss_sum, (1, LANES))], axis=0
+    )
+    own = jnp.pad(
+        slot_colors.reshape(3, devices, per_device).transpose(1, 0, 2),
+        ((0, 0), (0, 4), (0, LANES - per_device)),
+    )
+    message = jnp.concatenate(
+        [jnp.broadcast_to(shared[None], (devices,) + shared.shape), own], axis=1
+    )
+    in_vmem = pl.BlockSpec(memory_space=pltpu.VMEM)
+    dma = pltpu.SemaphoreType.DMA
+    sums, colors, head = pl.pallas_call(
+        functools.partial(tail_kernel, groups, shards),
+        in_specs=[in_vmem] * 3,
+        out_specs=[in_vmem] * 3,
+        out_shape=[
+            jax.ShapeDtypeStruct(message.shape[1:], jnp.float32),
+            jax.ShapeDtypeStruct((devices, 8, LANES), jnp.float32),
+            jax.ShapeDtypeStruct((groups, rows // groups, model), jnp.float32),
+        ],
+        scratch_shapes=[
+            pltpu.VMEM(message.shape, jnp.float32),
+            pltpu.VMEM(turned.shape, jnp.bfloat16),
+            pltpu.VMEM((shards, tokens, model), jnp.bfloat16),
+            pltpu.VMEM((groups, rows // groups, model), jnp.bfloat16),
+            pltpu.VMEM((groups, rows // groups, model), jnp.bfloat16),
+            pltpu.VMEM((groups, rows // groups, model), jnp.bfloat16),
+            dma((devices,)),
+            dma((devices,)),
+            dma((shards,)),
+            dma((shards,)),
+            dma((shards,)),
+            dma((shards,)),
+            dma((shards,)),
+            dma((groups,)),
+            dma((groups,)),
+            dma((groups,)),
+            dma((groups,)),
+        ],
+        compiler_params=pltpu.CompilerParams(collective_id=1, has_side_effects=True),
+    )(message, turned, d_field)
+    gain = sums[:gain_rows].reshape(model)
+    loss = sums[gain_rows, 0]
+    returned = colors[:, 1:4, :per_device].transpose(1, 0, 2).reshape(3, devices * per_device)
+    return returned, loss, head.reshape(rows, model), gain
+
+
 def body(
     latents,
     head_weight,
@@ -248,10 +532,6 @@
         w_second,
         color_head,
     )
-    returned = lax.all_to_all(
-        slot_colors, ("grp", "shard"), split_axis=1, concat_axis=1, tiled=True
-    )
-    rendered = returned[:, slot_of_ray]
     d_field = jnp.concatenate(
         [grad_first.reshape(per_layer, model), grad_second.reshape(per_layer, model)], axis=0
     ).astype(jnp.bfloat16)
@@ -261,18 +541,11 @@
         (((1,), (1,)), ((), ())),
         preferred_element_type=jnp.float32,
     )
-    columns = x_norm
-    group_part = lax.psum_scatter(
-        lax.dot_general(
-            columns, d_field, (((0,), (0,)), ((), ())), preferred_element_type=jnp.float32
-        ).astype(jnp.bfloat16),
-        "shard",
-        scatter_dimension=0,
-        tiled=True,
-    )
-    head_grad = jnp.sum(lax.all_gather(group_part, "grp", axis=0).astype(jnp.float32), axis=0)
     gain_part = jnp.sum(d_norm * x_hat, axis=0)
-    norm_gain_grad, loss_total = lax.psum((gain_part, loss_sum), ("grp", "shard"))
+    returned, loss_total, head_grad, norm_gain_grad = tail_exchange(
+        lax.axis_size("grp"), lax.axis_size("shard"), x_norm, d_field, gain_part, loss_sum, slot_colors
+    )
+    rendered = returned[:, slot_of_ray]
     d_scaled = d_norm * norm_gain
     latent_grad = (
         inv_rms * (d_scaled - x_hat * jnp.mean(d_scaled * x_hat, axis=1, keepdims=True))

time: 183 us -> 138 us (0.75)
  waiting for transfers between devices: 57.1 us -> 15.9 us
  blocking collectives: 40.9 us -> 0 us
  Pallas kernels: 29.1 us -> 68.5 us
  local copies, waits for them, and re-layouts: 11.6 us -> 17 us
  starting transfers between devices: 12 us -> 7.36 us
  matrix products: 5.12 us -> 3.02 us
    reduce_scatter x1 -> x0, waiting for transfers between devices: 41.2 us -> none  [body(): lax.psum_scatter(lax.dot_general(columns, d_field, (((0,), (0,)), ((), ()...]
    psum x1 -> x0, blocking collectives: 40.9 us -> none  [body(): lax.psum((gain_part, loss_sum), ('grp', 'shard'))]
    pallas_call x0 -> x1, Pallas kernels: none -> 39.3 us  [tail_exchange(): pl.pallas_call(functools.partial(tail_kernel, groups, shards), in_specs=[...]
    all_to_all x1 -> x0, starting transfers between devices: 4.59 us -> none  [body(): lax.all_to_all(slot_colors, ('grp', 'shard'), split_axis=1, concat_axis=1...]
    reduce_sum x1 -> x0, other arithmetic: 2.25 us -> none  [body(): jnp.sum(lax.all_gather(group_part, 'grp', axis=0).astype(jnp.float32), ax...]
    dot_general x1 -> x0, matrix products: 2.1 us -> none  [body(): lax.dot_general(columns, d_field, (((0,), (0,)), ((), ())), preferred_ele...]
    unnamed x16 -> x19, local copies, waits for them, and re-layouts: 1.6 us -> 3.49 us
  transfers between devices with their start and end apart: 5 -> 2, of which waited for: 3 -> 2; matrix products, arithmetic and copies ran while one was open for 10% -> 9% of each run, Pallas kernels for 0% -> 0%
where the time goes in v2:
time: 138 us; the launch traced here: 137 us
  Pallas kernels  68.5 us (50%)
  local copies, waits for them, and re-layouts  17 us (12%)
  waiting for transfers between devices  15.9 us (12%)
  between operations  15.6 us (11%)
  other arithmetic  9.43 us (7%)
  starting transfers between devices  7.36 us (5%)
  matrix products  3.02 us (2%)
    pallas_call x1, Pallas kernels, tail_exchange(): pl.pallas_call(functools.partial(tail_kernel, groups, shards), in_specs=[...  39.3 us
    pallas_call x1, Pallas kernels, render_slots(): pl.pallas_call(functools.partial(ray_kernel, ray_depth), grid=(total // b...  29.1 us
    all_to_all x1, waiting for transfers between devices, body(): lax.all_to_all(send, ('grp', 'shard'), split_axis=0, concat_axis=0, tiled...  9.97 us
    all_to_all x1, starting transfers between devices, body(): lax.all_to_all(send, ('grp', 'shard'), split_axis=0, concat_axis=0, tiled...  7.33 us
    all_gather x1, waiting for transfers between devices, body(): lax.all_gather(head_weight, 'shard', axis=0, tiled=True)  5.29 us
    unnamed x19, local copies, waits for them, and re-layouts  3.49 us
  transfers between devices with their start and end apart: 2, of which 2 were waited for; matrix products, arithmetic and copies ran while one was open for 9% of the time, Pallas kernels for 0%

profile of v2, /device:TPU:0, one launch (start us, length us, event | category | flops | bytes accessed | tf_op | source)
XLA Modules:
  0.0 136.9 jit_solution(14414220446396105276)
XLA Ops:
  7.2 0.7 all-gather.2.cloned.1.call-update
  7.9 0.8 copy.51
  8.7 0.8 convert_reduce_fusion
  9.6 0.7 compare_select_fusion
  10.2 1.9 %scatter_custom_fusion = f32[256,260]{1,0:T(8,128)} fusion(s32[64]{0:T(128)S(1)} %compare_select_fusion, f32[]{:T(128)} %constant.10.clone.1, f32[64,3]{1,0:T(8,128)S(1)} %copy.51, f32[]{:T(128)} %constant.34, f32[64,64]{1,0:T(8,128)} %param.13, f32[64,192]{1,0:T(8,128)} %param.12, f32[260]{0:T(512)S(1)} %pad.16.clone), kind=kCustom, calls=%fused_computation.19 | custom fusion | flops 49920 | bytes 366600 | tf_op jit(solution)/shard_map/scatter | solution.py:517
  12.2 7.3 %all-to-all-start = ((f32[32,8,260]{2,1,0:T(8,128)}), f32[32,8,260]{2,1,0:T(8,128)S(1)}, u32[]{:S(2)}, u32[]{:S(2)}) async-start(f32[32,8,260]{2,1,0:T(8,128)} %bitcast.1), calls=%async_computation | async-start | bytes 786432 | tf_op jit(solution)/shard_map/all_to_all | solution.py:518
  19.5 0.8 copy.57
  21.0 0.6 pad_bitcast_fusion.head_t_ref
  21.7 1.1 fusion.10
  22.8 10.0 %all-to-all-done = f32[32,8,260]{2,1,0:T(8,128)S(1)} async-done(((f32[32,8,260]{2,1,0:T(8,128)}), f32[32,8,260]{2,1,0:T(8,128)S(1)}, u32[]{:S(2)}, u32[]{:S(2)}) %all-to-all-start) | async-done | bytes 266272 | tf_op jit(solution)/shard_map/all_to_all | solution.py:518
  32.9 0.7 slice_reduce_fusion.1
  34.7 0.7 copy.58.factor_ref
  35.7 0.9 reshape.82.points_ref
  36.9 0.8 reshape.84.target_ref
  37.7 0.7 reshape.83.spacing_ref
  38.4 5.3 %all-gather.2.cloned.1.call-done = bf16[1024,1024]{1,0:T(8,128)(2,1)} async-done(((bf16[128,1024]{1,0:T(8,128)(2,1)}), bf16[1024,1024]{1,0:T(8,128)(2,1)}) %all-gather.2.cloned.1.call-update) | async-done | bytes 2097168 | tf_op jit(solution)/shard_map/all_gather | solution.py:503
  43.7 2.1 %convolution_convert_fusion = bf16[128,1024]{1,0:T(8,128)(2,1)S(1)} fusion(bf16[1024,1024]{1,0:T(8,128)(2,1)} %all-gather.2.cloned.1.call-done, bf16[128,1024]{1,0:T(8,128)(2,1)S(1)} %copy-done.1, f32[1024]{0:T(1024)S(1)} %copy-done.5, f32[128]{0:T(128)S(1)} %add_rsqrt_fusion), kind=kOutput, calls=%fused_computation.2 | convolution fusion | flops 269090816 | bytes 2626048 | tf_op jit(solution)/shard_map/dot_general | solution.py:501
  45.9 0.7 copy.59.second_t_ref
  46.7 0.8 copy.56
  47.5 29.1 %shard_map.119 = (f32[3,128,128]{2,1,0:T(8,128)}, f32[16,128]{1,0:T(8,128)}, f32[48,256]{1,0:T(8,128)}, f32[256,256]{1,0:T(8,128)}) custom-call(f32[3,16384]{1,0:T(4,128)} %reshape.82.points_ref, f32[128,128]{1,0:T(8,128)} %reshape.83.spacing_ref, f32[3,128,128]{2,1,0:T(8,128)} %reshape.84.target_ref, f32[128,128]{1,0:T(8,128)} %copy.58.factor_ref, ...), custom_call_target="tpu_custom_call" | custom-call | tf_op jit(solution)/shard_map/pallas_call | solution.py:148
  76.6 0.8 convert.11
  77.6 1.0 convert.12
  78.7 0.9 fusion.6
  79.7 0.9 fusion.9
  80.6 0.8 copy.62
  83.2 0.7 select_maximum_fusion.message_ref
  83.9 39.3 %shard_map.120 = (f32[16,128]{1,0:T(8,128)}, f32[32,8,128]{2,1,0:T(8,128)}, f32[4,32,1024]{2,1,0:T(8,128)}) custom-call(f32[32,16,128]{2,1,0:T(8,128)} %select_maximum_fusion.message_ref, bf16[8,128,128]{2,1,0:T(8,128)(2,1)} %bitcast.39, bf16[128,1024]{1,0:T(8,128)(2,1)} %copy-done.2), custom_call_target="tpu_custom_call" | custom-call | tf_op jit(solution)/shard_map/pallas_call | solution.py:443
  123.3 1.3 slice_bitcast_fusion.2
  124.5 1.2 slice.43
  125.7 0.9 slice_bitcast_fusion.1
  127.5 0.7 copy.65
  128.1 1.9 %copy.73 = f32[128,1024]{1,0:T(8,128)} copy(f32[128,1024]{1,0:T(8,128)} %bitcast.42) | data formatting | bytes 1048576
  (50 shorter events, 4.2 us)
Async XLA Ops:
  7.2 36.5 %all-gather.2.cloned.1.call-start = ((), (), s32[]{:S(2)}) async-start(), calls=%async_computation.1 | async-start | bytes 2359296 | tf_op jit(solution)/shard_map/all_gather | solution.py:503
  12.2 20.6 %all-to-all-start = ((f32[32,8,260]{2,1,0:T(8,128)}), f32[32,8,260]{2,1,0:T(8,128)S(1)}, u32[]{:S(2)}, u32[]{:S(2)}) async-start(f32[32,8,260]{2,1,0:T(8,128)} %bitcast.1), calls=%async_computation | async-start | bytes 786432 | tf_op jit(solution)/shard_map/all_to_all | solution.py:518
  32.8 10.9 %copy-start.1 = (bf16[128,1024]{1,0:T(8,128)(2,1)S(1)}, bf16[128,1024]{1,0:T(8,128)(2,1)}, u32[]{:S(2)}) copy-start(bf16[128,1024]{1,0:T(8,128)(2,1)} %param.8) | copy-start | bytes 786436
  32.8 10.9 %copy-start.5 = (f32[1024]{0:T(1024)S(1)}, f32[1024]{0:T(1024)}, u32[]{:S(2)}) copy-start(f32[1024]{0:T(1024)} %param.10) | copy-start | bytes 12292
  45.8 32.9 %copy-start = (bf16[1024,1024]{1,0:T(8,128)(2,1)S(1)}, bf16[1024,1024]{1,0:T(8,128)(2,1)}, u32[]{:S(2)}) copy-start(bf16[1024,1024]{1,0:T(8,128)(2,1)} %all-gather.2.cloned.1.call-done) | copy-start | bytes 6291460
  45.9 1.6 %copy-start.3 = (bf16[256,256]{1,0:T(8,128)(2,1)}, bf16[256,256]{1,0:T(8,128)(2,1)S(1)}, u32[]{:S(2)}) copy-start(bf16[256,256]{1,0:T(8,128)(2,1)S(1)} %reshape.86.second_ref) | copy-start | bytes 393220
  78.7 1.9 %copy-start.2 = (bf16[128,1024]{1,0:T(8,128)(2,1)}, bf16[128,1024]{1,0:T(8,128)(2,1)S(1)}, u32[]{:S(2)}) copy-start(bf16[128,1024]{1,0:T(8,128)(2,1)S(1)} %constant_dynamic-update-slice_fusion.field_ref) | copy-start | bytes 786436
  78.7 2.7 %copy-start.6 = (f32[16,128]{1,0:T(8,128)S(1)}, f32[16,128]{1,0:T(8,128)}, u32[]{:S(2)}) copy-start(f32[16,128]{1,0:T(8,128)} %get-tuple-element.14) | copy-start | bytes 24580
  78.7 3.3 %copy-start.4 = (f32[3,128,128]{2,1,0:T(8,128)S(1)}, f32[3,128,128]{2,1,0:T(8,128)}, u32[]{:S(2)}) copy-start(f32[3,128,128]{2,1,0:T(8,128)} %get-tuple-element.15) | copy-start | bytes 589828
Sparse Core Ops, SparseCore 0:
  9.9 33.7 all-gather.1

commit v3 on v2

--- a/solution.py
+++ b/solution.py
@@ -265,15 +265,12 @@
     colors_ref,
     head_ref,
     landed,
-    turned,
     fields,
     part,
     parts,
     done,
     message_sent,
     message_arrived,
-    turned_sent,
-    turned_arrived,
     field_sent,
     passed_on,
     field_arrived,
@@ -315,38 +312,15 @@
             partner,
         )
 
-    def turned_to(other):
-        return remote(
-            turned_ref.at[other],
-            turned.at[shard],
-            turned_sent.at[other],
-            turned_arrived.at[shard],
-            group,
-            other,
-        )
-
-    def turned_from(other):
-        return remote(
-            turned_ref.at[other],
-            turned.at[other],
-            turned_sent.at[other],
-            turned_arrived.at[other],
-            group,
-            other,
-        )
-
     greet_all(groups, shards)
     start_messages, finish_messages = messages(
         groups, shards, message_ref, landed, message_sent, message_arrived
     )
     peers = [lax.rem(chip + step, chips) * 2 + core for step in range(1, chips)]
     origins = [lax.rem(chip + chips - step, chips) * 2 + core for step in range(1, chips)]
-    others = [lax.rem(shard + step, shards) for step in range(1, shards)]
     for other in peers:
         field_to(other).start()
     field_to(partner).start()
-    for other in others:
-        turned_to(other).start()
     start_messages()
 
     def product(rows, field):
@@ -354,18 +328,15 @@
 
     total = product(turned_ref[shard], field_ref[...])
     field_pass(partner).wait_recv()
-    turned_from(partner).wait_recv()
-    total = total + product(turned[partner], fields[partner])
+    total = total + product(turned_ref[partner], fields[partner])
     for origin in origins:
         field_pass(origin).wait_recv()
         field_pass(origin).start()
-        turned_from(origin).wait_recv()
-        total = total + product(turned[origin], fields[origin])
+        total = total + product(turned_ref[origin], fields[origin])
     for origin in origins:
         across = origin + 1 - 2 * core
         field_pass(across).wait_recv()
-        turned_from(across).wait_recv()
-        total = total + product(turned[across], fields[across])
+        total = total + product(turned_ref[across], fields[across])
 
     part[...] = total.astype(jnp.bfloat16).reshape(part.shape)
     group_steps = [lax.rem(group + step, groups) for step in range(1, groups)]
@@ -414,20 +385,17 @@
     field_to(partner).wait_send()
     for origin in origins:
         field_pass(origin).wait_send()
-    for other in others:
-        turned_to(other).wait_send()
     for other in group_steps:
         part_to(other).wait_send()
         done_to(other).wait_send()
 
 
-def tail_exchange(groups, shards, x_norm, d_field, gain_part, loss_sum, slot_colors):
-    tokens, model = x_norm.shape
+def tail_exchange(groups, shards, turned, d_field, gain_part, loss_sum, slot_colors):
+    tokens, model = d_field.shape
     devices = groups * shards
     rows = model // shards
     gain_rows = model // LANES
     per_device = slot_colors.shape[1] // devices
-    turned = x_norm.T.reshape(shards, rows, tokens)
     shared = jnp.concatenate(
         [gain_part.reshape(gain_rows, LANES), jnp.broadcast_to(loss_sum, (1, LANES))], axis=0
     )
@@ -451,7 +419,6 @@
         ],
         scratch_shapes=[
             pltpu.VMEM(message.shape, jnp.float32),
-            pltpu.VMEM(turned.shape, jnp.bfloat16),
             pltpu.VMEM((shards, tokens, model), jnp.bfloat16),
             pltpu.VMEM((groups, rows // groups, model), jnp.bfloat16),
             pltpu.VMEM((groups, rows // groups, model), jnp.bfloat16),
@@ -461,8 +428,6 @@
             dma((shards,)),
             dma((shards,)),
             dma((shards,)),
-            dma((shards,)),
-            dma((shards,)),
             dma((groups,)),
             dma((groups,)),
             dma((groups,)),
@@ -474,6 +439,164 @@
     loss = sums[gain_rows, 0]
     returned = colors[:, 1:4, :per_device].transpose(1, 0, 2).reshape(3, devices * per_device)
     return returned, loss, head.reshape(rows, model), gain
+
+
+def start_kernel(
+    groups,
+    shards,
+    message_ref,
+    turned_ref,
+    weight_ref,
+    received_ref,
+    turned_all_ref,
+    weight_all_ref,
+    field_ref,
+    landed,
+    turned,
+    weights,
+    message_sent,
+    message_arrived,
+    turned_sent,
+    turned_arrived,
+    weight_sent,
+    passed_on,
+    weight_arrived,
+):
+    group = lax.axis_index("grp")
+    shard = lax.axis_index("shard")
+    me = group * shards + shard
+    chips = shards // 2
+    chip = shard // 2
+    core = lax.rem(shard, 2)
+    partner = chip * 2 + 1 - core
+
+    def remote(source, target, send_sem, recv_sem, to_shard):
+        return pltpu.make_async_remote_copy(
+            src_ref=source,
+            dst_ref=target,
+            send_sem=send_sem,
+            recv_sem=recv_sem,
+            device_id=(group, to_shard),
+            device_id_type=MESH,
+        )
+
+    def weight_to(other):
+        return remote(
+            weight_ref, weights.at[shard], weight_sent.at[other], weight_arrived.at[shard], other
+        )
+
+    def weight_pass(origin):
+        return remote(
+            weights.at[origin],
+            weights.at[origin],
+            passed_on.at[origin],
+            weight_arrived.at[origin],
+            partner,
+        )
+
+    def turned_to(other):
+        return remote(
+            turned_ref.at[other],
+            turned.at[shard],
+            turned_sent.at[other],
+            turned_arrived.at[shard],
+            other,
+        )
+
+    def turned_from(other):
+        return remote(
+            turned_ref.at[other],
+            turned.at[other],
+            turned_sent.at[other],
+            turned_arrived.at[other],
+            other,
+        )
+
+    greet_all(groups, shards)
+    start_messages, finish_messages = messages(
+        groups, shards, message_ref, landed, message_sent, message_arrived
+    )
+    peers = [lax.rem(chip + step, chips) * 2 + core for step in range(1, chips)]
+    origins = [lax.rem(chip + chips - step, chips) * 2 + core for step in range(1, chips)]
+    others = [lax.rem(shard + step, shards) for step in range(1, shards)]
+    for other in peers:
+        weight_to(other).start()
+    weight_to(partner).start()
+    start_messages()
+    for other in others:
+        turned_to(other).start()
+
+    def product(rows, weight):
+        return lax.dot_general(
+            rows, weight, (((0,), (0,)), ((), ())), preferred_element_type=jnp.float32
+        )
+
+    total = product(turned_ref[shard], weight_ref[...])
+    weight_all_ref[shard] = weight_ref[...]
+    turned_all_ref[shard] = turned_ref[shard]
+    weight_pass(partner).wait_recv()
+    total = total + product(turned_ref[partner], weights[partner])
+    weight_all_ref[partner] = weights[partner]
+    for origin in origins:
+        weight_pass(origin).wait_recv()
+        weight_pass(origin).start()
+        total = total + product(turned_ref[origin], weights[origin])
+        weight_all_ref[origin] = weights[origin]
+    for origin in origins:
+        across = origin + 1 - 2 * core
+        weight_pass(across).wait_recv()
+        total = total + product(turned_ref[across], weights[across])
+        weight_all_ref[across] = weights[across]
+    field_ref[...] = total.astype(jnp.bfloat16)
+
+    finish_messages()
+    landed[me] = message_ref[me]
+    received_ref[...] = landed[...]
+    for other in others:
+        turned_from(other).wait_recv()
+        turned_all_ref[other] = turned[other]
+    for other in peers:
+        weight_to(other).wait_send()
+    weight_to(partner).wait_send()
+    for origin in origins:
+        weight_pass(origin).wait_send()
+    for other in others:
+        turned_to(other).wait_send()
+
+
+def start_exchange(groups, shards, x_norm, head_weight, send):
+    tokens, model = x_norm.shape
+    devices = groups * shards
+    rows = model // shards
+    turned = x_norm.T.reshape(shards, rows, tokens)
+    message = send.reshape(devices, send.shape[0] // devices, send.shape[1])
+    in_vmem = pl.BlockSpec(memory_space=pltpu.VMEM)
+    dma = pltpu.SemaphoreType.DMA
+    received, turned_all, weight_all, field = pl.pallas_call(
+        functools.partial(start_kernel, groups, shards),
+        in_specs=[in_vmem] * 3,
+        out_specs=[in_vmem] * 4,
+        out_shape=[
+            jax.ShapeDtypeStruct(message.shape, jnp.float32),
+            jax.ShapeDtypeStruct(turned.shape, jnp.bfloat16),
+            jax.ShapeDtypeStruct((shards, rows, model), jnp.bfloat16),
+            jax.ShapeDtypeStruct((tokens, model), jnp.bfloat16),
+        ],
+        scratch_shapes=[
+            pltpu.VMEM(message.shape, jnp.float32),
+            pltpu.VMEM(turned.shape, jnp.bfloat16),
+            pltpu.VMEM((shards, rows, model), jnp.bfloat16),
+            dma((devices,)),
+            dma((devices,)),
+            dma((shards,)),
+            dma((shards,)),
+            dma((shards,)),
+            dma((shards,)),
+            dma((shards,)),
+        ],
+        compiler_params=pltpu.CompilerParams(collective_id=2, has_side_effects=True),
+    )(message, turned, head_weight)
+    return received.reshape(send.shape), turned_all, weight_all.reshape(model, model), field
 
 
 def body(
@@ -497,15 +620,6 @@
     inv_rms = lax.rsqrt(jnp.mean(latent_f32 * latent_f32, axis=1, keepdims=True) + norm_eps)
     x_hat = latent_f32 * inv_rms
     x_norm = (x_hat * norm_gain).astype(jnp.bfloat16)
-    columns = x_norm
-    field_sum = jnp.dot(
-        columns,
-        lax.all_gather(head_weight, "shard", axis=0, tiled=True),
-        preferred_element_type=jnp.float32,
-    )
-    field_rows = field_sum.astype(jnp.bfloat16)
-    w_first = field_rows[:per_layer].reshape(field_width, field_width)
-    w_second = field_rows[per_layer:].reshape(field_width, field_width)
     ray_ids = jnp.arange(ray_count, dtype=jnp.int32)
     same_scene = ray_scene[:, None] == ray_scene[None, :]
     earlier = ray_ids[:, None] < ray_ids[None, :]
@@ -515,7 +629,11 @@
         [sample_points, sample_spacing, ray_targets.T, jnp.ones((ray_count, 1), jnp.float32)], axis=1
     )
     send = jnp.zeros((slot_total, payload.shape[1]), jnp.float32).at[slot_of_ray].set(payload)
-    received = lax.all_to_all(send, ("grp", "shard"), split_axis=0, concat_axis=0, tiled=True)
+    received, x_turned, full_weight, field_rows = start_exchange(
+        lax.axis_size("grp"), lax.axis_size("shard"), x_norm, head_weight, send
+    )
+    w_first = field_rows[:per_layer].reshape(field_width, field_width)
+    w_second = field_rows[per_layer:].reshape(field_width, field_width)
     recv_points = received[:, : 3 * ray_depth]
     recv_spacing = received[:, 3 * ray_depth : 4 * ray_depth]
     recv_target = received[:, 4 * ray_depth : 4 * ray_depth + 3]
@@ -537,13 +655,13 @@
     ).astype(jnp.bfloat16)
     d_norm = lax.dot_general(
         d_field,
-        lax.all_gather(head_weight, "shard", axis=0, tiled=True),
+        full_weight,
         (((1,), (1,)), ((), ())),
         preferred_element_type=jnp.float32,
     )
     gain_part = jnp.sum(d_norm * x_hat, axis=0)
     returned, loss_total, head_grad, norm_gain_grad = tail_exchange(
-        lax.axis_size("grp"), lax.axis_size("shard"), x_norm, d_field, gain_part, loss_sum, slot_colors
+        lax.axis_size("grp"), lax.axis_size("shard"), x_turned, d_field, gain_part, loss_sum, slot_colors
     )
     rendered = returned[:, slot_of_ray]
     d_scaled = d_norm * norm_gain

time: 138 us -> 129 us (0.935)
  Pallas kernels: 68.5 us -> 96.1 us
  waiting for transfers between devices: 15.9 us -> 0 us
  between operations: 15.6 us -> 2.28 us
  starting transfers between devices: 7.36 us -> 0 us
  matrix products: 3.02 us -> 0.95 us
  other arithmetic: 9.43 us -> 11.3 us
    pallas_call x0 -> x1, Pallas kernels: none -> 30.7 us  [start_exchange(): pl.pallas_call(functools.partial(start_kernel, groups, shards), in_specs=...]
    all_to_all x1 -> x0, waiting for transfers between devices: 9.97 us -> none  [body(): lax.all_to_all(send, ('grp', 'shard'), split_axis=0, concat_axis=0, tiled...]
    all_to_all x1 -> x0, starting transfers between devices: 7.33 us -> none  [body(): lax.all_to_all(send, ('grp', 'shard'), split_axis=0, concat_axis=0, tiled...]
    all_gather x1 -> x0, waiting for transfers between devices: 5.29 us -> none  [body(): lax.all_gather(head_weight, 'shard', axis=0, tiled=True)]
    pallas_call x1, Pallas kernels: 39.3 us -> 36.2 us  [tail_exchange(): pl.pallas_call(functools.partial(tail_kernel, groups, shards), in_specs=[...]
    dot_general x2 -> x1, matrix products: 3.02 us -> 0.95 us  [body(): lax.dot_general(d_field, full_weight, (((1,), (1,)), ((), ())), preferred...]
    unnamed x19 -> x27, local copies, waits for them, and re-layouts: 3.49 us -> 3.02 us
  transfers between devices with their start and end apart: 2 -> 0, of which waited for: 2 -> 0; matrix products, arithmetic and copies ran while one was open for 9% -> 0% of each run, Pallas kernels for 0% -> 0%
where the time goes in v3:
time: 129 us; the launch traced here: 128 us
  Pallas kernels  96.1 us (74%)
  local copies, waits for them, and re-layouts  17.4 us (13%)
  other arithmetic  11.3 us (9%)
  between operations  2.28 us (2%)
    pallas_call x1, Pallas kernels, tail_exchange(): pl.pallas_call(functools.partial(tail_kernel, groups, shards), in_specs=[...  36.2 us
    pallas_call x1, Pallas kernels, start_exchange(): pl.pallas_call(functools.partial(start_kernel, groups, shards), in_specs=...  30.7 us
    pallas_call x1, Pallas kernels, render_slots(): pl.pallas_call(functools.partial(ray_kernel, ray_depth), grid=(total // b...  29.1 us
    unnamed x27, local copies, waits for them, and re-layouts  3.02 us

profile of v3, /device:TPU:0, one launch (start us, length us, event | category | flops | bytes accessed | tf_op | source)
XLA Modules:
  0.0 128.1 jit_solution(1542231523892132488)
XLA Ops:
  0.6 1.1 fusion.10
  1.7 1.1 fusion.11
  2.8 0.8 copy.38
  3.7 0.8 convert_reduce_fusion
  4.5 0.7 compare_select_fusion
  5.1 0.8 copy.37
  6.0 1.9 %scatter_custom_fusion = f32[256,260]{1,0:T(8,128)} fusion(s32[64]{0:T(128)S(1)} %compare_select_fusion, f32[]{:T(128)} %constant.10.clone.1, f32[64,3]{1,0:T(8,128)S(1)} %copy.37, f32[]{:T(128)} %constant.35, f32[64,64]{1,0:T(8,128)} %param.13, f32[64,192]{1,0:T(8,128)} %param.12, f32[260]{0:T(512)S(1)} %pad.16.clone), kind=kCustom, calls=%fused_computation.19 | custom fusion | flops 49920 | bytes 366600 | tf_op jit(solution)/shard_map/scatter | solution.py:631
  7.9 30.7 %shard_map.119 = (f32[32,8,260]{2,1,0:T(8,128)}, bf16[8,128,128]{2,1,0:T(8,128)(2,1)}, bf16[8,128,1024]{2,1,0:T(8,128)(2,1)}, bf16[128,1024]{1,0:T(8,128)(2,1)}) custom-call(f32[32,8,260]{2,1,0:T(8,128)} %bitcast.34, bf16[8,128,128]{2,1,0:T(8,128)(2,1)} %bitcast.40, bf16[128,1024]{1,0:T(8,128)(2,1)} %weight_ref.1), custom_call_target="tpu_custom_call" | custom-call | tf_op jit(solution)/shard_map/pallas_call | solution.py:575
  38.7 1.7 %slice_reduce_fusion.1 = (f32[]{:T(128)}, f32[256,1]{1,0:T(8,128)S(1)}) fusion(f32[256,260]{1,0:T(8,128)} %bitcast.36), kind=kLoop, calls=%fused_computation.42 | loop fusion | flops 255 | bytes 2052 | tf_op jit(solution)/shard_map/reduce_sum | solution.py:641
  41.4 0.7 copy.46.factor_ref
  42.1 1.0 slice.47
  43.4 0.9 reshape.92.points_ref
  44.6 0.8 reshape.94.target_ref
  45.5 0.7 reshape.93.spacing_ref
  46.3 0.8 copy.47.second_t_ref
  47.2 0.8 copy.44
  48.1 0.6 pad_bitcast_fusion.head_t_ref
  48.8 0.6 pad.9.clone.head_ref
  49.4 29.1 %shard_map.120 = (f32[3,128,128]{2,1,0:T(8,128)}, f32[16,128]{1,0:T(8,128)}, f32[48,256]{1,0:T(8,128)}, f32[256,256]{1,0:T(8,128)}) custom-call(f32[3,16384]{1,0:T(4,128)} %reshape.92.points_ref, f32[128,128]{1,0:T(8,128)} %reshape.93.spacing_ref, f32[3,128,128]{2,1,0:T(8,128)} %reshape.94.target_ref, f32[128,128]{1,0:T(8,128)} %copy.46.factor_ref, ...), custom_call_target="tpu_custom_call" | custom-call | tf_op jit(solution)/shard_map/pallas_call | solution.py:148
  78.6 0.8 convert.11
  79.5 1.0 convert.12
  80.7 0.9 fusion.6
  81.6 0.9 fusion.9
  82.5 0.6 reduce_sum.58
  84.3 0.7 select_maximum_fusion.message_ref
  85.1 36.2 %shard_map.121 = (f32[16,128]{1,0:T(8,128)}, f32[32,8,128]{2,1,0:T(8,128)}, f32[4,32,1024]{2,1,0:T(8,128)}) custom-call(f32[32,16,128]{2,1,0:T(8,128)} %select_maximum_fusion.message_ref, bf16[8,128,128]{2,1,0:T(8,128)(2,1)} %get-tuple-element.23.turned_ref, bf16[128,1024]{1,0:T(8,128)(2,1)} %copy-done.2), custom_call_target="tpu_custom_call" | custom-call | tf_op jit(solution)/shard_map/pallas_call | solution.py:411
  121.3 0.9 slice_bitcast_fusion.1
  122.5 0.6 gather_fusion
  123.1 0.7 copy.52
  123.7 1.3 slice_bitcast_fusion.2
  125.0 1.2 slice.43
  126.2 1.9 %copy.63 = f32[128,1024]{1,0:T(8,128)} copy(f32[128,1024]{1,0:T(8,128)} %bitcast.43) | data formatting | bytes 1048576
  (53 shorter events, 2.4 us)
Async XLA Ops:
  38.7 5.6 %copy-start.4 = (f32[32,8,260]{2,1,0:T(8,128)S(1)}, f32[32,8,260]{2,1,0:T(8,128)}, u32[]{:S(2)}) copy-start(f32[32,8,260]{2,1,0:T(8,128)} %get-tuple-element.16) | copy-start | bytes 798724
  41.4 4.8 %copy-start.5 = (bf16[128,1024]{1,0:T(8,128)(2,1)S(1)}, bf16[128,1024]{1,0:T(8,128)(2,1)}, u32[]{:S(2)}) copy-start(bf16[128,1024]{1,0:T(8,128)(2,1)} %get-tuple-element.17) | copy-start | bytes 786436
  43.4 4.6 %copy-start.9 = (bf16[4,256]{1,0:T(4,128)(2,1)S(1)}, bf16[4,256]{1,0:T(4,128)(2,1)}, u32[]{:S(2)}) copy-start(bf16[4,256]{1,0:T(4,128)(2,1)} %param.11) | copy-start | bytes 6148
  46.3 3.1 %copy-start.3 = (bf16[256,256]{1,0:T(8,128)(2,1)}, bf16[256,256]{1,0:T(8,128)(2,1)S(1)}, u32[]{:S(2)}) copy-start(bf16[256,256]{1,0:T(8,128)(2,1)S(1)} %reshape.96.second_ref) | copy-start | bytes 393220
  46.3 34.3 %copy-start = (bf16[128,1024]{1,0:T(8,128)(2,1)S(1)}, bf16[128,1024]{1,0:T(8,128)(2,1)}, u32[]{:S(2)}) copy-start(bf16[128,1024]{1,0:T(8,128)(2,1)} %param.8) | copy-start | bytes 786436
  46.3 34.3 %copy-start.1 = (bf16[8,128,1024]{2,1,0:T(8,128)(2,1)S(1)}, bf16[8,128,1024]{2,1,0:T(8,128)(2,1)}, u32[]{:S(2)}) copy-start(bf16[8,128,1024]{2,1,0:T(8,128)(2,1)} %get-tuple-element.20) | copy-start | bytes 6291460
  46.3 34.3 %copy-start.7 = (f32[1024]{0:T(1024)S(1)}, f32[1024]{0:T(1024)}, u32[]{:S(2)}) copy-start(f32[1024]{0:T(1024)} %param.10) | copy-start | bytes 12292
  80.6 1.9 %copy-start.2 = (bf16[128,1024]{1,0:T(8,128)(2,1)}, bf16[128,1024]{1,0:T(8,128)(2,1)S(1)}, u32[]{:S(2)}) copy-start(bf16[128,1024]{1,0:T(8,128)(2,1)S(1)} %constant_dynamic-update-slice_fusion.field_ref) | copy-start | bytes 786436
  80.6 1.9 %copy-start.8 = (f32[16,128]{1,0:T(8,128)S(1)}, f32[16,128]{1,0:T(8,128)}, u32[]{:S(2)}) copy-start(f32[16,128]{1,0:T(8,128)} %get-tuple-element.21) | copy-start | bytes 24580
  80.7 3.2 %copy-start.6 = (f32[3,128,128]{2,1,0:T(8,128)S(1)}, f32[3,128,128]{2,1,0:T(8,128)}, u32[]{:S(2)}) copy-start(f32[3,128,128]{2,1,0:T(8,128)} %get-tuple-element.22) | copy-start | bytes 589828

commit v4 on v3

--- a/solution.py
+++ b/solution.py
@@ -11,6 +11,7 @@
 
 
 LANES = 128
+HALVES = 2
 SINE = (3.14159265358979, -5.16771278004997, 2.55016403987735, -0.599264529320792, 0.0821458866111282, -0.00737043094571435, 0.000466302805767613, -0.0000219153534478303)
 
 
@@ -31,13 +32,15 @@
     spacing_ref,
     target_ref,
     factor_ref,
+    first_ref,
+    second_ref,
+    head_ref,
+    color_ref,
+    loss_ref,
+    d_first_ref,
+    d_second_ref,
     first_t_ref,
     second_t_ref,
-    second_ref,
-    head_ref,
-    head_t_ref,
-    color_ref,
-    loss_ref,
     grad_first_ref,
     grad_second_ref,
     raw_ref,
@@ -53,7 +56,8 @@
         loss_ref[...] = jnp.zeros_like(loss_ref)
         grad_first_ref[...] = jnp.zeros_like(grad_first_ref)
         grad_second_ref[...] = jnp.zeros_like(grad_second_ref)
-        draw_ref[...] = jnp.zeros_like(draw_ref)
+        first_t_ref[...] = first_ref[...].T
+        second_t_ref[...] = second_ref[...].T
 
     feature = lax.broadcasted_iota(jnp.int32, (48, 1), 0)
     component = feature % 3
@@ -120,7 +124,9 @@
         for i in range(chunks):
             draw_ref[c : c + 1, i * LANES : (i + 1) * LANES] = value[i : i + 1, :]
     d_raw = draw_ref[...].astype(jnp.bfloat16)
-    d_htwo = product(head_t_ref[...], d_raw)
+    d_htwo = lax.dot_general(
+        head_ref[...], d_raw, (((0,), (0,)), ((), ())), preferred_element_type=jnp.float32
+    )
     d_atwo = (jnp.where(h_two > 0, d_htwo, 0.0) * fan_scale).astype(jnp.bfloat16)
     over_samples = (((1,), (1,)), ((), ()))
     grad_second_ref[...] += lax.dot_general(
@@ -131,6 +137,12 @@
     grad_first_ref[...] += lax.dot_general(
         distinct, d_aone, over_samples, preferred_element_type=jnp.float32
     )
+
+    @pl.when(pl.program_id(0) == pl.num_programs(0) - 1)
+    def _():
+        first = grad_first_ref[...].astype(jnp.bfloat16)
+        d_first_ref[...] = jnp.concatenate([first] * copies + [first[: width - 48 * copies]], axis=0)
+        d_second_ref[...] = grad_second_ref[...].astype(jnp.bfloat16)
 
 
 def render_slots(points, spacing, target, factor, w_first, w_second, color_head):
@@ -143,9 +155,8 @@
     flat_points = points.reshape(slots, 3, ray_depth).transpose(1, 0, 2).reshape(3, total)
     wide_target = jnp.broadcast_to(target.T[:, :, None], (3, slots, ray_depth)).reshape(3, rows, LANES)
     wide_factor = jnp.broadcast_to(factor[:, None], (slots, ray_depth)).reshape(rows, LANES)
-    head = jnp.pad(color_head, ((0, 16 - color_head.shape[0]), (0, 0)))
     fixed = lambda b: (0, 0)
-    color, loss, grad_distinct, grad_second = pl.pallas_call(
+    color, loss, grad_first, grad_second = pl.pallas_call(
         functools.partial(ray_kernel, ray_depth),
         grid=(total // block,),
         in_specs=[
@@ -155,40 +166,38 @@
             pl.BlockSpec((block_rows, LANES), lambda b: (b, 0)),
             pl.BlockSpec((width, width), fixed),
             pl.BlockSpec((width, width), fixed),
-            pl.BlockSpec((width, width), fixed),
-            pl.BlockSpec((16, width), fixed),
-            pl.BlockSpec((width, 16), fixed),
+            pl.BlockSpec(color_head.shape, fixed),
         ],
         out_specs=[
             pl.BlockSpec((3, block_rows, LANES), lambda b: (0, b, 0)),
             pl.BlockSpec((block_rows, LANES), fixed),
-            pl.BlockSpec((48, width), fixed),
+            pl.BlockSpec((width, width), fixed),
             pl.BlockSpec((width, width), fixed),
         ],
         out_shape=[
             jax.ShapeDtypeStruct((3, rows, LANES), jnp.float32),
             jax.ShapeDtypeStruct((block_rows, LANES), jnp.float32),
-            jax.ShapeDtypeStruct((48, width), jnp.float32),
-            jax.ShapeDtypeStruct((width, width), jnp.float32),
+            jax.ShapeDtypeStruct((width, width), jnp.bfloat16),
+            jax.ShapeDtypeStruct((width, width), jnp.bfloat16),
         ],
         scratch_shapes=[
+            pltpu.VMEM((width, width), jnp.bfloat16),
+            pltpu.VMEM((width, width), jnp.bfloat16),
+            pltpu.VMEM((48, width), jnp.float32),
+            pltpu.VMEM((width, width), jnp.float32),
             pltpu.VMEM((4, block_rows, LANES), jnp.float32),
-            pltpu.VMEM((16, block), jnp.float32),
+            pltpu.VMEM((4, block), jnp.float32),
         ],
     )(
         flat_points,
         spacing.reshape(rows, LANES),
         wide_target,
         wide_factor,
-        w_first.T,
-        w_second.T,
+        w_first,
         w_second,
-        head,
-        head.T,
+        color_head,
     )
     colors = color.reshape(3, slots, ray_depth)[:, :, 0]
-    copies = -(-width // 48)
-    grad_first = jnp.tile(grad_distinct, (copies, 1))[:width]
     return colors, jnp.sum(loss) * (1.0 / ray_depth), grad_first, grad_second
 
 
@@ -297,17 +306,27 @@
             device_id_type=MESH,
         )
 
-    def field_to(other):
-        return remote(
-            field_ref, fields.at[shard], field_sent.at[other], field_arrived.at[shard], group, other
-        )
-
-    def field_pass(origin):
-        return remote(
-            fields.at[origin],
-            fields.at[origin],
-            passed_on.at[origin],
-            field_arrived.at[origin],
+    width = field_ref.shape[1] // HALVES
+
+    def columns(half):
+        return pl.ds(half * width, width)
+
+    def field_to(half, other):
+        return remote(
+            field_ref.at[:, columns(half)],
+            fields.at[half, shard],
+            field_sent.at[half, other],
+            field_arrived.at[half, shard],
+            group,
+            other,
+        )
+
+    def field_pass(half, origin):
+        return remote(
+            fields.at[half, origin],
+            fields.at[half, origin],
+            passed_on.at[half, origin],
+            field_arrived.at[half, origin],
             group,
             partner,
         )
@@ -318,76 +337,107 @@
     )
     peers = [lax.rem(chip + step, chips) * 2 + core for step in range(1, chips)]
     origins = [lax.rem(chip + chips - step, chips) * 2 + core for step in range(1, chips)]
-    for other in peers:
-        field_to(other).start()
-    field_to(partner).start()
+    group_steps = [lax.rem(group + step, groups) for step in range(1, groups)]
+    for half in range(HALVES):
+        for other in peers:
+            field_to(half, other).start()
+        field_to(half, partner).start()
     start_messages()
 
     def product(rows, field):
         return jnp.dot(rows, field, preferred_element_type=jnp.float32)
 
-    total = product(turned_ref[shard], field_ref[...])
-    field_pass(partner).wait_recv()
-    total = total + product(turned_ref[partner], fields[partner])
-    for origin in origins:
-        field_pass(origin).wait_recv()
-        field_pass(origin).start()
-        total = total + product(turned_ref[origin], fields[origin])
-    for origin in origins:
-        across = origin + 1 - 2 * core
-        field_pass(across).wait_recv()
-        total = total + product(turned_ref[across], fields[across])
-
-    part[...] = total.astype(jnp.bfloat16).reshape(part.shape)
-    group_steps = [lax.rem(group + step, groups) for step in range(1, groups)]
-
-    def part_to(other):
-        return remote(
-            part.at[other], parts.at[group], part_sent.at[other], part_arrived.at[group], other, shard
-        )
-
-    def part_from(other):
-        return remote(
-            part.at[other], parts.at[other], part_sent.at[other], part_arrived.at[other], other, shard
-        )
-
-    def done_to(other):
-        return remote(
-            done.at[group], done.at[group], done_sent.at[other], done_arrived.at[group], other, shard
-        )
-
-    def done_from(other):
-        return remote(
-            done.at[other], done.at[other], done_sent.at[other], done_arrived.at[other], other, shard
-        )
-
-    for other in group_steps:
-        part_to(other).start()
-    slice_sum = part[group].astype(jnp.float32)
-    for other in group_steps:
-        part_from(other).wait_recv()
-        slice_sum = slice_sum + parts[other].astype(jnp.float32)
-    done[group] = slice_sum.astype(jnp.bfloat16)
-    for other in group_steps:
-        done_to(other).start()
-    head_ref[group] = slice_sum
+    def part_to(half, other):
+        return remote(
+            part.at[half, other],
+            parts.at[half, group],
+            part_sent.at[half, other],
+            part_arrived.at[half, group],
+            other,
+            shard,
+        )
+
+    def part_from(half, other):
+        return remote(
+            part.at[half, other],
+            parts.at[half, other],
+            part_sent.at[half, other],
+            part_arrived.at[half, other],
+            other,
+            shard,
+        )
+
+    def done_to(half, other):
+        return remote(
+            done.at[half, group],
+            done.at[half, group],
+            done_sent.at[half, other],
+            done_arrived.at[half, group],
+            other,
+            shard,
+        )
+
+    def done_from(half, other):
+        return remote(
+            done.at[half, other],
+            done.at[half, other],
+            done_sent.at[half, other],
+            done_arrived.at[half, other],
+            other,
+            shard,
+        )
+
+    def gather_half(half):
+        total = product(turned_ref[shard], field_ref[:, half * width : (half + 1) * width])
+        field_pass(half, partner).wait_recv()
+        total = total + product(turned_ref[partner], fields[half, partner])
+        for origin in origins:
+            field_pass(half, origin).wait_recv()
+            field_pass(half, origin).start()
+            total = total + product(turned_ref[origin], fields[half, origin])
+        for origin in origins:
+            across = origin + 1 - 2 * core
+            field_pass(half, across).wait_recv()
+            total = total + product(turned_ref[across], fields[half, across])
+        part[half] = total.astype(jnp.bfloat16).reshape(part.shape[1:])
+        for other in group_steps:
+            part_to(half, other).start()
+
+    def sum_half(half):
+        slice_sum = part[half, group].astype(jnp.float32)
+        for other in group_steps:
+            part_from(half, other).wait_recv()
+            slice_sum = slice_sum + parts[half, other].astype(jnp.float32)
+        done[half, group] = slice_sum.astype(jnp.bfloat16)
+        for other in group_steps:
+            done_to(half, other).start()
+        head_ref[group, :, half * width : (half + 1) * width] = slice_sum
+
+    for half in range(HALVES):
+        gather_half(half)
+        if half > 0:
+            sum_half(half - 1)
+    sum_half(HALVES - 1)
 
     finish_messages()
     landed[me] = message_ref[me]
     colors_ref[...] = landed[:, landed.shape[1] - 8 :, :]
     sums_ref[...] = jnp.sum(landed[...], axis=0)
 
-    for other in group_steps:
-        done_from(other).wait_recv()
-        head_ref[other] = done[other].astype(jnp.float32)
-    for other in peers:
-        field_to(other).wait_send()
-    field_to(partner).wait_send()
-    for origin in origins:
-        field_pass(origin).wait_send()
-    for other in group_steps:
-        part_to(other).wait_send()
-        done_to(other).wait_send()
+    for half in range(HALVES):
+        for other in group_steps:
+            done_from(half, other).wait_recv()
+            head_ref[other, :, half * width : (half + 1) * width] = done[half, other].astype(
+                jnp.float32
+            )
+        for other in peers:
+            field_to(half, other).wait_send()
+        field_to(half, partner).wait_send()
+        for origin in origins:
+            field_pass(half, origin).wait_send()
+        for other in group_steps:
+            part_to(half, other).wait_send()
+            done_to(half, other).wait_send()
 
 
 def tail_exchange(groups, shards, turned, d_field, gain_part, loss_sum, slot_colors):
@@ -419,19 +469,19 @@
         ],
         scratch_shapes=[
             pltpu.VMEM(message.shape, jnp.float32),
-            pltpu.VMEM((shards, tokens, model), jnp.bfloat16),
-            pltpu.VMEM((groups, rows // groups, model), jnp.bfloat16),
-            pltpu.VMEM((groups, rows // groups, model), jnp.bfloat16),
-            pltpu.VMEM((groups, rows // groups, model), jnp.bfloat16),
+            pltpu.VMEM((HALVES, shards, tokens, model // HALVES), jnp.bfloat16),
+            pltpu.VMEM((HALVES, groups, rows // groups, model // HALVES), jnp.bfloat16),
+            pltpu.VMEM((HALVES, groups, rows // groups, model // HALVES), jnp.bfloat16),
+            pltpu.VMEM((HALVES, groups, rows // groups, model // HALVES), jnp.bfloat16),
             dma((devices,)),
             dma((devices,)),
-            dma((shards,)),
-            dma((shards,)),
-            dma((shards,)),
-            dma((groups,)),
-            dma((groups,)),
-            dma((groups,)),
-            dma((groups,)),
+            dma((HALVES, shards)),
+            dma((HALVES, shards)),
+            dma((HALVES, shards)),
+            dma((HALVES, groups)),
+            dma((HALVES, groups)),
+            dma((HALVES, groups)),
+            dma((HALVES, groups)),
         ],
         compiler_params=pltpu.CompilerParams(collective_id=1, has_side_effects=True),
     )(message, turned, d_field)
@@ -652,7 +702,7 @@
     )
     d_field = jnp.concatenate(
         [grad_first.reshape(per_layer, model), grad_second.reshape(per_layer, model)], axis=0
-    ).astype(jnp.bfloat16)
+    )
     d_norm = lax.dot_general(
         d_field,
         full_weight,

time: 129 us -> 125 us (0.969)
  Pallas kernels: 96.1 us -> 91.5 us
  local copies, waits for them, and re-layouts: 17.4 us -> 19.3 us
    pallas_call x1, Pallas kernels: 36.2 us -> 31.6 us  [tail_exchange(): pl.pallas_call(functools.partial(tail_kernel, groups, shards), in_specs=[...]
    another operation x2 -> x0, other arithmetic: 1.77 us -> none
    transpose x2 -> x0, local copies, waits for them, and re-layouts: 1.39 us -> none  [render_slots(): color, loss, grad_distinct, grad_second = pl.pallas_call(functools.partia...]
    unnamed x27 -> x17, local copies, waits for them, and re-layouts: 3.02 us -> 2.76 us
where the time goes in v4:
time: 125 us; the launch traced here: 124 us
  Pallas kernels  91.5 us (73%)
  local copies, waits for them, and re-layouts  19.3 us (15%)
  other arithmetic  10.2 us (8%)
  between operations  2.17 us (2%)
    pallas_call x1, Pallas kernels, tail_exchange(): pl.pallas_call(functools.partial(tail_kernel, groups, shards), in_specs=[...  31.6 us
    pallas_call x1, Pallas kernels, start_exchange(): pl.pallas_call(functools.partial(start_kernel, groups, shards), in_specs=...  30.7 us
    pallas_call x1, Pallas kernels, render_slots(): pl.pallas_call(functools.partial(ray_kernel, ray_depth), grid=(total // b...  29.1 us
    unnamed x17, local copies, waits for them, and re-layouts  2.76 us

profile of v4, /device:TPU:0, one launch (start us, length us, event | category | flops | bytes accessed | tf_op | source)
XLA Modules:
  0.0 124.1 jit_solution(14302594915065280813)
XLA Ops:
  0.6 0.8 convert_reduce_fusion
  1.5 0.7 compare_select_fusion
  2.1 1.1 fusion.10
  3.3 0.8 copy.30
  4.1 1.1 fusion.11
  5.2 0.8 copy.31
  6.0 1.9 %scatter_custom_fusion = f32[256,260]{1,0:T(8,128)} fusion(s32[64]{0:T(128)S(1)} %compare_select_fusion, f32[]{:T(128)} %constant.9.clone.1, f32[64,3]{1,0:T(8,128)S(1)} %copy.30, f32[]{:T(128)} %constant.31, f32[64,64]{1,0:T(8,128)} %param.13, f32[64,192]{1,0:T(8,128)} %param.12, f32[260]{0:T(512)S(1)} %pad.11.clone), kind=kCustom, calls=%fused_computation.19 | custom fusion | flops 49920 | bytes 366600 | tf_op jit(solution)/shard_map/scatter | solution.py:681
  7.9 30.7 %shard_map.119 = (f32[32,8,260]{2,1,0:T(8,128)}, bf16[8,128,128]{2,1,0:T(8,128)(2,1)}, bf16[8,128,1024]{2,1,0:T(8,128)(2,1)}, bf16[128,1024]{1,0:T(8,128)(2,1)}) custom-call(f32[32,8,260]{2,1,0:T(8,128)} %bitcast.30, bf16[8,128,128]{2,1,0:T(8,128)(2,1)} %bitcast.35, bf16[128,1024]{1,0:T(8,128)(2,1)} %weight_ref.1), custom_call_target="tpu_custom_call" | custom-call | tf_op jit(solution)/shard_map/pallas_call | solution.py:625
  38.7 1.0 slice_bitcast_fusion
  39.7 1.0 slice.43
  40.7 0.7 reshape.87.spacing_ref
  41.4 1.6 %slice_reduce_fusion.1 = (f32[]{:T(128)}, f32[256,1]{1,0:T(8,128)S(1)}) fusion(f32[256,260]{1,0:T(8,128)} %bitcast.33), kind=kLoop, calls=%fused_computation.42 | loop fusion | flops 255 | bytes 2052 | tf_op jit(solution)/shard_map/reduce_sum | solution.py:691
  43.7 1.0 slice.42
  45.2 0.7 copy.37.factor_ref
  46.1 0.9 reshape.86.points_ref
  47.0 0.7 reshape.90.second_ref
  47.8 0.7 reshape.89.first_ref
  48.7 0.8 reshape.88.target_ref
  49.5 29.1 %shard_map.120 = (f32[3,128,128]{2,1,0:T(8,128)}, f32[16,128]{1,0:T(8,128)}, bf16[256,256]{1,0:T(8,128)(2,1)}, bf16[256,256]{1,0:T(8,128)(2,1)}) custom-call(f32[3,16384]{1,0:T(4,128)} %reshape.86.points_ref, f32[128,128]{1,0:T(8,128)} %reshape.87.spacing_ref, f32[3,128,128]{2,1,0:T(8,128)} %reshape.88.target_ref, f32[128,128]{1,0:T(8,128)} %copy.37.factor_ref, ...), custom_call_target="tpu_custom_call" | custom-call | tf_op jit(solution)/shard_map/pallas_call | solution.py:159
  78.6 1.3 %reduce_sum.58 = f32[]{:T(128)} reduce(f32[16,128]{1,0:T(8,128)} %get-tuple-element.21, f32[]{:T(128)} %constant.9.clone.1), dimensions={0,1}, to_apply=%region_5.0 | reduce | flops 2047 | bytes 8200 | tf_op jit(solution)/shard_map/reduce_sum | solution.py:201
  80.5 1.0 reshape.91
  81.6 1.0 reshape.92
  82.6 0.9 fusion.6
  83.6 0.9 fusion.9
  85.0 0.7 select_maximum_fusion.message_ref
  85.7 31.6 %shard_map.121 = (f32[16,128]{1,0:T(8,128)}, f32[32,8,128]{2,1,0:T(8,128)}, f32[4,32,1024]{2,1,0:T(8,128)}) custom-call(f32[32,16,128]{2,1,0:T(8,128)} %select_maximum_fusion.message_ref, bf16[8,128,128]{2,1,0:T(8,128)(2,1)} %get-tuple-element.23.turned_ref, bf16[128,1024]{1,0:T(8,128)(2,1)} %copy-done.2), custom_call_target="tpu_custom_call" | custom-call | tf_op jit(solution)/shard_map/pallas_call | solution.py:461
  117.4 1.2 slice.38
  118.5 0.9 slice_bitcast_fusion.1
  119.5 1.3 %slice_bitcast_fusion.2 = f32[1024]{0:T(1024)} fusion(f32[16,128]{1,0:T(8,128)} %get-tuple-element.25), kind=kLoop, calls=%fused_computation.37 | loop fusion | bytes 8192 | tf_op jit(solution)/shard_map/reshape | solution.py:488
  121.0 0.6 gather_fusion
  121.6 0.7 copy.41
  122.2 1.9 %copy.51 = f32[128,1024]{1,0:T(8,128)} copy(f32[128,1024]{1,0:T(8,128)} %bitcast.37) | data formatting | bytes 1048576
  (35 shorter events, 1.7 us)
Async XLA Ops:
  38.7 8.3 %copy-start.3 = (bf16[128,1024]{1,0:T(8,128)(2,1)S(1)}, bf16[128,1024]{1,0:T(8,128)(2,1)}, u32[]{:S(2)}) copy-start(bf16[128,1024]{1,0:T(8,128)(2,1)} %get-tuple-element.17) | copy-start | bytes 786436
  47.0 35.6 %copy-start = (bf16[128,1024]{1,0:T(8,128)(2,1)S(1)}, bf16[128,1024]{1,0:T(8,128)(2,1)}, u32[]{:S(2)}) copy-start(bf16[128,1024]{1,0:T(8,128)(2,1)} %param.8) | copy-start | bytes 786436
  47.0 35.6 %copy-start.1 = (bf16[8,128,1024]{2,1,0:T(8,128)(2,1)S(1)}, bf16[8,128,1024]{2,1,0:T(8,128)(2,1)}, u32[]{:S(2)}) copy-start(bf16[8,128,1024]{2,1,0:T(8,128)(2,1)} %get-tuple-element.20) | copy-start | bytes 6291460
  47.0 35.6 %copy-start.5 = (f32[1024]{0:T(1024)S(1)}, f32[1024]{0:T(1024)}, u32[]{:S(2)}) copy-start(f32[1024]{0:T(1024)} %param.10) | copy-start | bytes 12292
  82.6 1.9 %copy-start.2 = (bf16[128,1024]{1,0:T(8,128)(2,1)}, bf16[128,1024]{1,0:T(8,128)(2,1)S(1)}, u32[]{:S(2)}) copy-start(bf16[128,1024]{1,0:T(8,128)(2,1)S(1)} %constant_dynamic-update-slice_fusion.field_ref) | copy-start | bytes 786436
  82.6 1.9 %copy-start.4 = (f32[3,128,128]{2,1,0:T(8,128)S(1)}, f32[3,128,128]{2,1,0:T(8,128)}, u32[]{:S(2)}) copy-start(f32[3,128,128]{2,1,0:T(8,128)} %get-tuple-element.22) | copy-start | bytes 589828
